TPU v7x, 256 devices: a whole 4x4x8 slice. The times are simulated.
256 devices in a mesh: dp: 16 (over y, z_hi), expert: 8 (over x, core), tensor: 2 (over z_lo).
Axes of the slice: x: 4, y: 4, z: 8 (z_hi: 4, z_lo: 2; z = z_hi * 2 + z_lo), core: 2. Of those that a mesh axis runs over, the one named last changes fastest.
Arguments:
- tokens: bfloat16 [2048, 5120], P('dp', 'tensor'), may hold values from -6 to 6
- routes: int32 [2048, 6], P('dp'), may hold values from 0 to 15, all different within a row; in each aligned block of 128 rows (0 to 127, 128 to 255, ...) at most 72 rows name the same one
- route_weights: float32 [2048, 6], P('dp'), may hold values from 0.05 to 0.5
- gate_weight: bfloat16 [16, 1536, 5120], P('dp', 'expert', 'tensor'), may hold values from -0.078125 to 0.078125
- up_weight: bfloat16 [16, 1536, 5120], P('dp', 'expert', 'tensor'), may hold values from -0.078125 to 0.078125
- down_weight: bfloat16 [16, 1536, 5120], P('dp', 'expert', 'tensor'), may hold values from -0.15625 to 0.15625
- cotangent: bfloat16 [2048, 5120], P('dp', 'tensor'), may hold values from -6 to 6
Outputs:
- layer_out: bfloat16 [2048, 5120], P('dp', 'tensor')
- token_grad: bfloat16 [2048, 5120], P('dp', 'tensor')
- gate_grad: float32 [16, 1536, 5120], P('dp', 'expert', 'tensor')
- up_grad: float32 [16, 1536, 5120], P('dp', 'expert', 'tensor')
- down_grad: float32 [16, 1536, 5120], P('dp', 'expert', 'tensor')
Inputs may be any that keep to these rules, and one draw needn't show every extreme that they name: `routes`: each row names 6 different experts. In the rows of one index of dp (aligned blocks of 128 rows) no expert is named by more than 72 rows, a bound that some block reaches.
All inputs are finite; a program needn't handle non-finite values.
Results may differ from a plain program's by a relative error of at most 0.023.
Values may be sent and summed in bfloat16 or wider, within the bound.
A program may use at most 128 MiB of HBM per device.

v0:
```python
import jax
import jax.numpy as jnp
from jax import lax
from jax.sharding import PartitionSpec as P


def body(tokens, routes, route_weights, gate_weight, up_weight, down_weight, cotangent):
    dp_count = lax.axis_size("dp")
    hidden_split = lax.axis_size("expert")
    local_exp, hidden_share, half_width = gate_weight.shape
    tok_rows, top_count = routes.shape
    experts = local_exp * dp_count
    capacity = min(tok_rows, 3 * tok_rows * top_count // (2 * experts))
    share_rows = capacity // hidden_split
    pair_count = tok_rows * top_count
    slot_count = experts * capacity
    flat_route = routes.reshape(pair_count)
    onehot = (flat_route[:, None] == jnp.arange(experts, dtype=jnp.int32)[None, :]).astype(
        jnp.int32
    )
    position = jnp.sum((jnp.cumsum(onehot, axis=0) - 1) * onehot, axis=1)
    target = flat_route * capacity + position
    selector = jnp.arange(slot_count, dtype=jnp.int32)[:, None] == target[None, :]
    place_tok = jnp.any(selector.reshape(slot_count, tok_rows, top_count), axis=2).astype(
        jnp.bfloat16
    )
    flat_weight = route_weights.reshape(pair_count)
    slot_weight = jnp.sum(jnp.where(selector, flat_weight[None, :], jnp.float32(0.0)), axis=1)
    pair_token = jnp.arange(pair_count, dtype=jnp.int32) // top_count
    slot_token = jnp.sum(jnp.where(selector, pair_token[None, :], 0), axis=1)
    slot_used = jnp.any(selector, axis=1)
    slot_token = jnp.where(slot_used, slot_token, tok_rows)
    own_start = lax.axis_index("expert") * share_rows
    own_place = lax.dynamic_slice_in_dim(
        place_tok.reshape(experts, capacity, tok_rows), own_start, share_rows, 1
    )
    own_place = own_place.reshape(experts * share_rows, tok_rows)
    own_weight = lax.dynamic_slice_in_dim(
        slot_weight.reshape(experts, capacity), own_start, share_rows, 1
    )
    own_weight = own_weight.reshape(experts * share_rows)
    own_token = lax.dynamic_slice_in_dim(
        slot_token.reshape(experts, capacity), own_start, share_rows, 1
    )
    own_token = own_token.reshape(experts * share_rows)

    def send_rows(slot_rows):
        slot_grid = slot_rows.reshape(dp_count, local_exp, capacity, half_width)
        arrived = lax.all_to_all(slot_grid, "dp", split_axis=0, concat_axis=2, tiled=True)
        return arrived.reshape(local_exp, dp_count, capacity, half_width)

    def width_sum(partial_values):
        return lax.psum(partial_values.astype(jnp.bfloat16), "tensor").astype(jnp.float32)

    def reduce_rows(partial_rows):
        slot_grid = partial_rows.reshape(local_exp, dp_count, capacity, half_width)
        summed = lax.psum_scatter(
            slot_grid.astype(jnp.bfloat16), "expert", scatter_dimension=2, tiled=True
        )
        return summed

    def send_home(share_block):
        returned = lax.all_to_all(share_block, "dp", split_axis=1, concat_axis=0, tiled=True)
        return returned.reshape(experts * share_rows, half_width)

    def token_sum(partial_tokens):
        return lax.psum(partial_tokens.astype(jnp.bfloat16), "expert").astype(jnp.float32)

    token_slots = jnp.dot(place_tok, tokens, preferred_element_type=jnp.float32).astype(
        jnp.bfloat16
    )
    rows = send_rows(token_slots)
    flat_rows = rows.reshape(local_exp, dp_count * capacity, half_width)
    gate_part = jnp.einsum(
        "lrd,lfd->lrf", flat_rows, gate_weight, preferred_element_type=jnp.float32
    )
    up_part = jnp.einsum("lrd,lfd->lrf", flat_rows, up_weight, preferred_element_type=jnp.float32)
    both_values = width_sum(jnp.stack((gate_part, up_part)))
    gate_val = both_values[0]
    up_val = both_values[1]
    sigmoid_gate = jax.nn.sigmoid(gate_val)
    activated = gate_val * sigmoid_gate
    hidden = (activated * up_val).astype(jnp.bfloat16)
    down_part = jnp.einsum("lrf,lfd->lrd", hidden, down_weight, preferred_element_type=jnp.float32)
    expert_out = send_home(reduce_rows(down_part))
    weighted = own_weight[:, None] * expert_out.astype(jnp.float32)
    out_part = (
        jnp.zeros((tok_rows, half_width), jnp.float32).at[own_token].add(weighted, mode="drop")
    )
    layer_out = token_sum(out_part).astype(jnp.bfloat16)
    pair_grad = (
        flat_weight[:, None] * jnp.repeat(cotangent, top_count, axis=0).astype(jnp.float32)
    ).astype(jnp.bfloat16)
    grad_slots = jnp.dot(
        selector.astype(jnp.bfloat16), pair_grad, preferred_element_type=jnp.float32
    ).astype(jnp.bfloat16)
    grad_rows = send_rows(grad_slots).reshape(local_exp, dp_count * capacity, half_width)
    hidden_grad = width_sum(
        jnp.einsum("lrd,lfd->lrf", grad_rows, down_weight, preferred_element_type=jnp.float32)
    )
    gate_delta = (
        hidden_grad * up_val * sigmoid_gate * (1.0 + gate_val * (1.0 - sigmoid_gate))
    ).astype(jnp.bfloat16)
    up_delta = (hidden_grad * activated).astype(jnp.bfloat16)
    input_part = jnp.einsum(
        "lrf,lfd->lrd", gate_delta, gate_weight, preferred_element_type=jnp.float32
    )
    input_part = input_part + jnp.einsum(
        "lrf,lfd->lrd", up_delta, up_weight, preferred_element_type=jnp.float32
    )
    row_grad = send_home(reduce_rows(input_part))
    grad_part = jnp.einsum("st,sd->td", own_place, row_grad, preferred_element_type=jnp.float32)
    token_grad = token_sum(grad_part).astype(jnp.bfloat16)
    gate_grad = jnp.einsum(
        "lrf,lrd->lfd", gate_delta, flat_rows, preferred_element_type=jnp.float32
    )
    up_grad = jnp.einsum("lrf,lrd->lfd", up_delta, flat_rows, preferred_element_type=jnp.float32)
    down_grad = jnp.einsum("lrf,lrd->lfd", hidden, grad_rows, preferred_element_type=jnp.float32)
    return (layer_out, token_grad, gate_grad, up_grad, down_grad)


def solution(mesh):
    in_specs = (
        P("dp", "tensor"),
        P("dp", None),
        P("dp", None),
        P("dp", "expert", "tensor"),
        P("dp", "expert", "tensor"),
        P("dp", "expert", "tensor"),
        P("dp", "tensor"),
    )
    out_specs = (
        P("dp", "tensor"),
        P("dp", "tensor"),
        P("dp", "expert", "tensor"),
        P("dp", "expert", "tensor"),
        P("dp", "expert", "tensor"),
    )
    return jax.shard_map(body, mesh=mesh, in_specs=in_specs, out_specs=out_specs, check_vma=False)
```

profile of v0, /device:TPU:1, one launch (start us, length us, event | category | flops | bytes accessed | tf_op | source)
XLA Modules:
  0.0 625.3 jit_solution(9417354293102109201)
XLA Ops:
  7.2 0.9 copy.48
  8.1 0.1 reshape.331
  8.2 0.1 eq.47
  8.4 1.7 reduce-window.6
  10.1 0.3 slice_reduce_fusion
  10.3 0.1 fusion.34
  10.4 0.1 reduce_sum.32
  10.6 0.1 copy.52
  10.6 0.7 multiply_add_fusion
  11.4 0.6 fusion.4
  12.0 5.4 convolution_convert_fusion.1
  17.3 11.9 %all-to-all-start = ((bf16[16,1,72,2560]{3,2,1,0:T(8,128)(2,1)}), bf16[16,1,72,2560]{3,2,1,0:T(8,128)(2,1)}, u32[]{:S(2)}, u32[]{:S(2)}) async-start(bf16[16,1,72,2560]{3,2,1,0:T(8,128)(2,1)} %bitcast.114), calls=%async_computation | async-start | bytes 11796480 | tf_op jit(solution)/shard_map/all_to_all | solution.py:49
  29.3 0.1 copy.51
  29.4 0.1 broadcast_in_dim.45
  29.5 5.3 broadcast_in_dim.48
  34.9 9.5 %convert_element_type.111 = f32[768,2560]{1,0:T(8,128)} reshape(f32[128,6,2560]{2,1,0:T(8,128)} %broadcast_in_dim.48) | data formatting | bytes 15728640 | tf_op jit(solution)/shard_map/convert_element_type | solution.py:92
  44.4 9.9 %convolution_convert_fusion = bf16[1152,2560]{1,0:T(8,128)(2,1)} fusion(f32[768,2560]{1,0:T(8,128)} %convert_element_type.111, f32[768]{0:T(1024)S(1)} %broadcast_in_dim.45, s32[768]{0:T(1024)S(1)} %get-tuple-element.10), kind=kOutput, calls=%fused_computation.2 | convolution fusion | flops 4537614336 | bytes 13768704 | tf_op jit(solution)/shard_map/dot_general | solution.py:94
  54.3 105.5 %all-to-all-done = bf16[16,1,72,2560]{3,2,1,0:T(8,128)(2,1)} async-done(((bf16[16,1,72,2560]{3,2,1,0:T(8,128)(2,1)}), bf16[16,1,72,2560]{3,2,1,0:T(8,128)(2,1)}, u32[]{:S(2)}, u32[]{:S(2)}) %all-to-all-start) | async-done | bytes 5898272 | tf_op jit(solution)/shard_map/all_to_all | solution.py:49
  159.8 8.0 %all-to-all-start.2 = ((bf16[16,1,72,2560]{3,2,1,0:T(8,128)(2,1)}), bf16[16,1,72,2560]{3,2,1,0:T(8,128)(2,1)}, u32[]{:S(2)}, u32[]{:S(2)}) async-start(bf16[16,1,72,2560]{3,2,1,0:T(8,128)(2,1)} %bitcast.116), calls=%async_computation.3 | async-start | bytes 11796480 | tf_op jit(solution)/shard_map/all_to_all | solution.py:49
  167.8 5.1 fusion.6
  172.9 4.7 fusion.5
  177.7 1.0 pad_maximum_fusion
  178.7 92.0 %all-to-all-done.2 = bf16[16,1,72,2560]{3,2,1,0:T(8,128)(2,1)} async-done(((bf16[16,1,72,2560]{3,2,1,0:T(8,128)(2,1)}), bf16[16,1,72,2560]{3,2,1,0:T(8,128)(2,1)}, u32[]{:S(2)}, u32[]{:S(2)}) %all-to-all-start.2) | async-done | bytes 5898272 | tf_op jit(solution)/shard_map/all_to_all | solution.py:49
  270.7 5.5 fusion.7
  276.2 0.2 reduce-scatter.3.cloned.1.call-start
  276.4 125.8 %all-reduce.7.cloned.1.call-done = (bf16[2,1,1152,192]{2,3,1,0:T(8,128)(2,1)}, bf16[1,1152,192]{1,2,0:T(8,128)(2,1)}) async-done(((bf16[2,1,1152,192]{2,3,1,0:T(8,128)(2,1)}, bf16[1,1152,192]{1,2,0:T(8,128)(2,1)}), (bf16[2,1,1152,192]{2,3,1,0:T(8,128)(2,1)}, bf16[1,1152,192]{1,2,0:T(8,128)(2,1)})) %all-reduce.7.cloned.1.call-update) | async-done | bytes 1327120 | tf_op jit(solution)/shard_map/psum | solution.py:53
  402.3 1.3 convert_element_type.102
  403.5 0.3 multiply_convert_fusion.2
  403.8 1.1 copy.54
  404.9 2.8 fusion.1
  407.6 4.3 copy.55
  412.0 0.9 copy-done.2
  412.9 0.4 fusion.20
  413.3 3.0 fusion.15
  416.4 1.9 fusion
  418.2 4.4 copy.58
  422.6 32.5 %reduce-scatter.3.cloned.1.call-done = bf16[1,16,9,2560]{3,1,0,2:T(8,128)(2,1)} async-done(((bf16[1,16,72,2560]{3,1,0,2:T(8,128)(2,1)}), bf16[1,16,9,2560]{3,1,0,2:T(8,128)(2,1)}) %reduce-scatter.3.cloned.1.call-update) | async-done | bytes 737296 | tf_op jit(solution)/shard_map/reduce_scatter | solution.py:57
  455.1 2.6 copy.56
  457.7 9.3 %all-to-all-start.1 = ((bf16[1,16,9,2560]{3,2,0,1:T(8,128)(2,1)}), bf16[1,16,9,2560]{3,2,0,1:T(8,128)(2,1)}, u32[]{:S(2)}, u32[]{:S(2)}) async-start(bf16[1,16,9,2560]{3,2,0,1:T(8,128)(2,1)} %copy.56), calls=%async_computation.2 | async-start | bytes 2621440 | tf_op jit(solution)/shard_map/all_to_all | solution.py:63
  467.1 0.5 fusion.3
  467.5 0.4 select_reduce_fusion.1
  468.0 33.4 %reduce-scatter.5.cloned.1.call-done = bf16[1,16,9,2560]{3,1,0,2:T(8,128)(2,1)} async-done(((bf16[1,16,72,2560]{3,1,0,2:T(8,128)(2,1)}), bf16[1,16,9,2560]{3,1,0,2:T(8,128)(2,1)}) %reduce-scatter.5.cloned.1.call-update) | async-done | bytes 737296 | tf_op jit(solution)/shard_map/reduce_scatter | solution.py:57
  501.3 2.6 copy.59
  503.9 9.3 %all-to-all-start.3 = ((bf16[1,16,9,2560]{3,2,0,1:T(8,128)(2,1)}), bf16[1,16,9,2560]{3,2,0,1:T(8,128)(2,1)}, u32[]{:S(2)}, u32[]{:S(2)}) async-start(bf16[1,16,9,2560]{3,2,0,1:T(8,128)(2,1)} %copy.59), calls=%async_computation.5 | async-start | bytes 2621440 | tf_op jit(solution)/shard_map/all_to_all | solution.py:63
  513.3 0.1 select_n.43
  513.4 0.1 constant_dynamic-slice_fusion.1
  513.5 0.1 reshape.333
  513.6 0.4 select_reduce_fusion
  514.0 0.1 reshape.334
  514.1 0.1 constant_dynamic-slice_fusion
  514.2 0.1 mul.95
  514.3 0.8 constant_dynamic-slice_fusion.2
  515.2 5.4 convolution_bitcast_fusion
  520.6 2.7 reshape.347
  523.3 4.7 scatter_custom_fusion
  528.0 2.2 convert_element_type.109
  530.2 15.4 %all-to-all-done.3 = bf16[1,16,9,2560]{3,2,0,1:T(8,128)(2,1)} async-done(((bf16[1,16,9,2560]{3,2,0,1:T(8,128)(2,1)}), bf16[1,16,9,2560]{3,2,0,1:T(8,128)(2,1)}, u32[]{:S(2)}, u32[]{:S(2)}) %all-to-all-start.3) | async-done | bytes 737312 | tf_op jit(solution)/shard_map/all_to_all | solution.py:63
  545.6 1.6 reshape.346
  547.2 1.2 convolution_convert_fusion.3
  548.5 5.4 convolution_bitcast_fusion.2
  553.9 5.5 convolution_bitcast_fusion.1
  559.4 55.4 %all-reduce.5.cloned.1.call-done = (bf16[128,2560]{1,0:T(8,128)(2,1)}, bf16[128,2560]{1,0:T(8,128)(2,1)}) async-done(((bf16[128,2560]{1,0:T(8,128)(2,1)}, bf16[128,2560]{1,0:T(8,128)(2,1)}), (bf16[128,2560]{1,0:T(8,128)(2,1)}, bf16[128,2560]{1,0:T(8,128)(2,1)})) %all-reduce.5.cloned.1.call-update) | async-done | bytes 1310736 | tf_op jit(solution)/shard_map/psum | solution.py:67
  614.8 2.0 copy.66
  616.8 2.0 copy.67
  (31 shorter events, 0.3 us)
Async XLA Ops:
  7.2 263.5 %copy-start = (bf16[1,192,2560]{2,1,0:T(8,128)(2,1)S(1)}, bf16[1,192,2560]{2,1,0:T(8,128)(2,1)}, u32[]{:S(2)}) copy-start(bf16[1,192,2560]{2,1,0:T(8,128)(2,1)} %param.12) | copy-start | bytes 2949124
  12.0 5.4 copy-start.4
  17.3 11.9 %copy-start.8 = (f32[128,6]{0,1:T(8,128)S(1)}, f32[128,6]{0,1:T(8,128)}, u32[]{:S(2)}) copy-start(f32[128,6]{0,1:T(8,128)} %param.9) | copy-start | bytes 9220
  17.3 12.2 %copy-start.7 = (bf16[128,2560]{1,0:T(8,128)(2,1)S(1)}, bf16[128,2560]{1,0:T(8,128)(2,1)}, u32[]{:S(2)}) copy-start(bf16[128,2560]{1,0:T(8,128)(2,1)} %param.13) | copy-start | bytes 1966084
  17.3 142.5 %all-to-all-start = ((bf16[16,1,72,2560]{3,2,1,0:T(8,128)(2,1)}), bf16[16,1,72,2560]{3,2,1,0:T(8,128)(2,1)}, u32[]{:S(2)}, u32[]{:S(2)}) async-start(bf16[16,1,72,2560]{3,2,1,0:T(8,128)(2,1)} %bitcast.114), calls=%async_computation | async-start | bytes 11796480 | tf_op jit(solution)/shard_map/all_to_all | solution.py:49
  159.8 110.9 %all-to-all-start.2 = ((bf16[16,1,72,2560]{3,2,1,0:T(8,128)(2,1)}), bf16[16,1,72,2560]{3,2,1,0:T(8,128)(2,1)}, u32[]{:S(2)}, u32[]{:S(2)}) async-start(bf16[16,1,72,2560]{3,2,1,0:T(8,128)(2,1)} %bitcast.116), calls=%async_computation.3 | async-start | bytes 11796480 | tf_op jit(solution)/shard_map/all_to_all | solution.py:49
  167.8 234.5 %all-reduce.7.cloned.1.call-start = ((), (), s32[]{:S(2)}) async-start(), calls=%async_computation.9 | async-start | bytes 2654208 | tf_op jit(solution)/shard_map/psum | solution.py:53
  167.8 5.1 copy-start.5
  276.2 178.9 %reduce-scatter.3.cloned.1.call-start = ((), (), s32[]{:S(2)}) async-start(), calls=%async_computation.6 | async-start | bytes 6635520 | tf_op jit(solution)/shard_map/reduce_scatter | solution.py:57
  411.9 1.0 copy-start.2
  412.0 89.4 %reduce-scatter.5.cloned.1.call-start = ((), (), s32[]{:S(2)}) async-start(), calls=%async_computation.7 | async-start | bytes 6635520 | tf_op jit(solution)/shard_map/reduce_scatter | solution.py:57
  413.3 3.0 copy-start.6
  457.7 46.2 %all-to-all-start.1 = ((bf16[1,16,9,2560]{3,2,0,1:T(8,128)(2,1)}), bf16[1,16,9,2560]{3,2,0,1:T(8,128)(2,1)}, u32[]{:S(2)}, u32[]{:S(2)}) async-start(bf16[1,16,9,2560]{3,2,0,1:T(8,128)(2,1)} %copy.56), calls=%async_computation.2 | async-start | bytes 2621440 | tf_op jit(solution)/shard_map/all_to_all | solution.py:63
  503.9 41.7 %all-to-all-start.3 = ((bf16[1,16,9,2560]{3,2,0,1:T(8,128)(2,1)}), bf16[1,16,9,2560]{3,2,0,1:T(8,128)(2,1)}, u32[]{:S(2)}, u32[]{:S(2)}) async-start(bf16[1,16,9,2560]{3,2,0,1:T(8,128)(2,1)} %copy.59), calls=%async_computation.5 | async-start | bytes 2621440 | tf_op jit(solution)/shard_map/all_to_all | solution.py:63
  513.3 101.5 %all-reduce.5.cloned.1.call-start = ((), (), s32[]{:S(2)}) async-start(), calls=%async_computation.8 | async-start | bytes 2621440 | tf_op jit(solution)/shard_map/psum | solution.py:67
  548.5 5.4 copy-start.3
  553.9 64.8 %copy-start.1 = (bf16[1,192,2560]{2,1,0:T(8,128)(2,1)S(1)}, bf16[1,192,2560]{2,1,0:T(8,128)(2,1)}, u32[]{:S(2)}) copy-start(bf16[1,192,2560]{2,1,0:T(8,128)(2,1)} %param.12) | copy-start | bytes 2949124
Sparse Core Ops, SparseCore 0:
  276.3 125.8 all-reduce.6
  412.1 42.9 reduce-scatter.2
  457.7 43.6 reduce-scatter.4
  548.6 66.1 all-reduce.4
where the time goes:
time: 628 us; the launch traced here: 625 us
  waiting for transfers between devices  460 us (73%)
  matrix products  55.7 us (9%)
  local copies, waits for them, and re-layouts  42.2 us (7%)
  starting transfers between devices  38.9 us (6%)
  other arithmetic  14.3 us (2%)
  between operations  14 us (2%)
    all_to_all x2, waiting for transfers between devices, send_rows(): lax.all_to_all(slot_grid, 'dp', split_axis=0, concat_axis=2, tiled=True)  198 us
    psum x1, waiting for transfers between devices, width_sum(): lax.psum(partial_values.astype(jnp.bfloat16), 'tensor').astype(jnp.float32)  126 us
    reduce_scatter x2, waiting for transfers between devices, reduce_rows(): lax.psum_scatter(slot_grid.astype(jnp.bfloat16), 'expert', scatter_dimens...  65.9 us
    psum x1, waiting for transfers between devices, token_sum(): lax.psum(partial_tokens.astype(jnp.bfloat16), 'expert').astype(jnp.float32)  55.4 us
    all_to_all x2, starting transfers between devices, send_rows(): lax.all_to_all(slot_grid, 'dp', split_axis=0, concat_axis=2, tiled=True)  19.9 us
    all_to_all x2, starting transfers between devices, send_home(): lax.all_to_all(share_block, 'dp', split_axis=1, concat_axis=0, tiled=True)  18.7 us
    all_to_all x2, waiting for transfers between devices, send_home(): lax.all_to_all(share_block, 'dp', split_axis=1, concat_axis=0, tiled=True)  15.4 us
  transfers between devices with their start and end apart: 8, of which 7 were waited for; matrix products, arithmetic and copies ran while one was open for 13% of the time, Pallas kernels for 0%

commit v1 on v0

v1 whole, which is shorter than its diff:
```python
import jax
import jax.numpy as jnp
from jax import lax
from jax.sharding import PartitionSpec as P


def body(tokens, routes, route_weights, gate_weight, up_weight, down_weight, cotangent):
    dp_count = lax.axis_size("dp")
    hidden_split = lax.axis_size("expert")
    gate_weight, up_weight, down_weight = gate_weight[0], up_weight[0], down_weight[0]
    hidden_share, half_width = gate_weight.shape
    tok_rows, top_count = routes.shape
    experts = dp_count
    capacity = min(tok_rows, 3 * tok_rows * top_count // (2 * experts))
    share_rows = capacity // hidden_split
    own_rows = experts * share_rows
    pair_count = tok_rows * top_count

    flat_route = routes.T.reshape(pair_count)
    onehot = (flat_route[:, None] == jnp.arange(experts, dtype=jnp.int32)[None, :])
    running = jnp.cumsum(onehot.astype(jnp.int32), axis=0) - 1
    position = jnp.sum(jnp.where(onehot, running, 0), axis=1)
    target = flat_route * capacity + position
    member = lax.axis_index("expert")
    own_index = jnp.arange(own_rows, dtype=jnp.int32)
    own_slot = (own_index // share_rows) * capacity + member * share_rows + own_index % share_rows
    selector = (own_slot[:, None] == target[None, :]).reshape(own_rows, top_count, tok_rows)
    weight_grid = jnp.sum(
        jnp.where(selector, route_weights.T[None], jnp.float32(0.0)), axis=1
    )
    own_weight = jnp.sum(weight_grid, axis=1, keepdims=True)
    own_place = jnp.any(selector, axis=1).astype(jnp.bfloat16)

    def select(values):
        return jnp.dot(own_place, values, preferred_element_type=jnp.float32)

    def dispatch(rows):
        arrived = lax.all_to_all(
            rows.reshape(dp_count, share_rows, half_width), "dp", split_axis=0, concat_axis=0, tiled=True
        )
        return lax.all_gather(
            arrived.reshape(own_rows, half_width), "expert", axis=0, tiled=True
        )

    def width_sum(partial_values):
        mine = partial_values.astype(jnp.bfloat16)
        other = lax.ppermute(mine, "tensor", [(0, 1), (1, 0)])
        return mine.astype(jnp.float32) + other.astype(jnp.float32)

    def home(partial_rows):
        summed = lax.psum_scatter(
            partial_rows.astype(jnp.bfloat16), "expert", scatter_dimension=0, tiled=True
        )
        returned = lax.all_to_all(
            summed.reshape(dp_count, share_rows, half_width), "dp", split_axis=0, concat_axis=0, tiled=True
        )
        return returned.reshape(own_rows, half_width)

    def token_sum(partial_tokens):
        part = lax.psum_scatter(
            partial_tokens.astype(jnp.bfloat16), "expert", scatter_dimension=0, tiled=True
        )
        return lax.all_gather(part, "expert", axis=0, tiled=True)

    rows = dispatch(select(tokens).astype(jnp.bfloat16))
    grad_rows = dispatch((select(cotangent) * own_weight).astype(jnp.bfloat16))

    nt = (((1,), (1,)), ((), ()))
    nn = (((1,), (0,)), ((), ()))
    tn = (((0,), (0,)), ((), ()))

    def mm(a, b, dims):
        return lax.dot_general(a, b, dims, preferred_element_type=jnp.float32)

    gate_val = width_sum(mm(rows, gate_weight, nt))
    up_val = width_sum(mm(rows, up_weight, nt))
    sigmoid_gate = jax.nn.sigmoid(gate_val)
    activated = gate_val * sigmoid_gate
    hidden = (activated * up_val).astype(jnp.bfloat16)
    expert_out = home(mm(hidden, down_weight, nn))
    out_part = mm(weight_grid.astype(jnp.bfloat16), expert_out, tn)
    layer_out = token_sum(out_part)

    hidden_grad = width_sum(mm(grad_rows, down_weight, nt))
    gate_delta = (
        hidden_grad * up_val * sigmoid_gate * (1.0 + gate_val * (1.0 - sigmoid_gate))
    ).astype(jnp.bfloat16)
    up_delta = (hidden_grad * activated).astype(jnp.bfloat16)
    input_part = mm(gate_delta, gate_weight, nn) + mm(up_delta, up_weight, nn)
    row_grad = home(input_part)
    token_grad = token_sum(mm(own_place, row_grad, tn))
    gate_grad = mm(gate_delta, rows, tn)
    up_grad = mm(up_delta, rows, tn)
    down_grad = mm(hidden, grad_rows, tn)
    return (layer_out, token_grad, gate_grad[None], up_grad[None], down_grad[None])


def solution(mesh):
    in_specs = (
        P("dp", "tensor"),
        P("dp", None),
        P("dp", None),
        P("dp", "expert", "tensor"),
        P("dp", "expert", "tensor"),
        P("dp", "expert", "tensor"),
        P("dp", "tensor"),
    )
    out_specs = (
        P("dp", "tensor"),
        P("dp", "tensor"),
        P("dp", "expert", "tensor"),
        P("dp", "expert", "tensor"),
        P("dp", "expert", "tensor"),
    )
    return jax.shard_map(body, mesh=mesh, in_specs=in_specs, out_specs=out_specs, check_vma=False)
```

time: 628 us -> 378 us (0.60)
  waiting for transfers between devices: 460 us -> 165 us
  blocking collectives: 0 us -> 111 us
  local copies, waits for them, and re-layouts: 42.2 us -> 15.4 us
  matrix products: 55.7 us -> 38.2 us
  starting transfers between devices: 38.9 us -> 25.7 us
  other arithmetic: 14.3 us -> 6.83 us
    all_to_all x4 -> x2, waiting for transfers between devices: 213 us -> 29.5 us  [home(): lax.all_to_all(summed.reshape(dp_count, share_rows, half_width), 'dp', sp...]
    psum x2 -> x0, waiting for transfers between devices: 181 us -> none  [the longest x1 126 us: width_sum(): lax.psum(partial_values.astype(jnp.bfloat16), 'tensor').astype(jnp.float32)]
    all_to_all x0 -> x2, blocking collectives: none -> 78 us  [dispatch(): lax.all_to_all(rows.reshape(dp_count, share_rows, half_width), 'dp', spli...]
    all_gather x0 -> x2, waiting for transfers between devices: none -> 37.2 us  [dispatch(): lax.all_gather(arrived.reshape(own_rows, half_width), 'expert', axis=0, t...]
    all_gather x0 -> x2, blocking collectives: none -> 33.3 us  [token_sum(): return lax.all_gather(part, 'expert', axis=0, tiled=True)]
    convert_element_type x5 -> x0, local copies, waits for them, and re-layouts: 21.9 us -> none  [the longest x1 9.49 us: body(): jnp.repeat(cotangent, top_count, axis=0).astype(jnp.float32)]
    all_to_all x4 -> x2, starting transfers between devices: 38.5 us -> 18.6 us  [home(): lax.all_to_all(summed.reshape(dp_count, share_rows, half_width), 'dp', sp...]
    dot_general x12 -> x13, matrix products: 55.7 us -> 38.2 us  [the longest x11 35.3 us: mm(): return lax.dot_general(a, b, dims, preferred_element_type=jnp.float32)]
  transfers between devices with their start and end apart: 8 -> 11, of which waited for: 7 -> 8; matrix products, arithmetic and copies ran while one was open for 13% -> 11% of each run, Pallas kernels for 0% -> 0%
where the time goes in v1:
time: 378 us; the launch traced here: 377 us
  waiting for transfers between devices  165 us (44%)
  blocking collectives  111 us (29%)
  matrix products  38.2 us (10%)
  starting transfers between devices  25.7 us (7%)
  local copies, waits for them, and re-layouts  15.4 us (4%)
  between operations  14.4 us (4%)
  other arithmetic  6.83 us (2%)
    all_to_all x2, blocking collectives, dispatch(): lax.all_to_all(rows.reshape(dp_count, share_rows, half_width), 'dp', spli...  78 us
    reduce_scatter x2, waiting for transfers between devices, home(): lax.psum_scatter(partial_rows.astype(jnp.bfloat16), 'expert', scatter_dim...  70.4 us
    all_gather x2, waiting for transfers between devices, dispatch(): lax.all_gather(arrived.reshape(own_rows, half_width), 'expert', axis=0, t...  37.2 us
    dot_general x11, matrix products, mm(): return lax.dot_general(a, b, dims, preferred_element_type=jnp.float32)  35.3 us
    all_gather x2, blocking collectives, token_sum(): return lax.all_gather(part, 'expert', axis=0, tiled=True)  33.3 us
    all_to_all x2, waiting for transfers between devices, home(): lax.all_to_all(summed.reshape(dp_count, share_rows, half_width), 'dp', sp...  29.5 us
    all_to_all x2, starting transfers between devices, home(): lax.all_to_all(summed.reshape(dp_count, share_rows, half_width), 'dp', sp...  18.6 us
    ppermute x3, waiting for transfers between devices, width_sum(): other = lax.ppermute(mine, 'tensor', [(0, 1), (1, 0)])  17.4 us
  transfers between devices with their start and end apart: 11, of which 8 were waited for; matrix products, arithmetic and copies ran while one was open for 11% of the time, Pallas kernels for 0%

profile of v1, /device:TPU:1, one launch (start us, length us, event | category | flops | bytes accessed | tf_op | source)
XLA Modules:
  0.0 376.8 jit_solution(5594621330869188232)
XLA Ops:
  7.2 0.0 copy-start
  7.2 0.0 all-gather.5.cloned.1.call-start
  7.2 0.8 fusion.12
  8.0 1.7 reduce-window.6
  9.7 0.3 slice_reduce_fusion
  10.0 0.8 fusion.11
  10.8 0.7 bitcast_add_fusion
  11.5 0.1 compare_reduce_fusion
  11.6 0.9 select_reduce_fusion
  12.5 1.4 fusion.1
  13.9 0.3 reshape.100
  14.2 45.1 %all_to_all.20 = bf16[16,9,2560]{2,1,0:T(8,128)(2,1)} all-to-all(bf16[16,9,2560]{2,1,0:T(8,128)(2,1)S(1)} %reshape.100), channel_id=1, replica_groups=mesh['dp'=16,'expert'=8,'tensor'=2] {'dp'}, dimensions={0} | all-to-all | bytes 1474560 | tf_op jit(solution)/shard_map/all_to_all | solution.py:38
  59.3 2.5 reshape.101
  61.8 0.0 all-gather.5.cloned.1.call-update
  61.8 0.0 all-gather.3.cloned.1.call-start
  61.9 1.4 convolution_convert_fusion.1
  63.3 0.3 reshape.96
  63.6 33.0 %all_to_all.21 = bf16[16,9,2560]{2,1,0:T(8,128)(2,1)} all-to-all(bf16[16,9,2560]{2,1,0:T(8,128)(2,1)S(1)} %reshape.96), channel_id=1, replica_groups=mesh['dp'=16,'expert'=8,'tensor'=2] {'dp'}, dimensions={0} | all-to-all | bytes 1474560 | tf_op jit(solution)/shard_map/all_to_all | solution.py:38
  96.6 2.5 reshape.97
  99.1 0.0 all-gather.3.cloned.1.call-update
  99.1 0.0 copy-start.7
  99.1 0.0 reduce-scatter.5.cloned.1.call-start
  99.1 2.7 all-gather.5.cloned.1.call-done
  101.9 4.7 %convolution_convert_fusion.4 = bf16[1152,192]{0,1:T(8,128)(2,1)S(1)} fusion(bf16[1152,2560]{1,0:T(8,128)(2,1)} %all-gather.5.cloned.1.call-done, bf16[1,192,2560]{2,1,0:T(8,128)(2,1)S(1)} %copy-done), kind=kOutput, calls=%fused_computation.11 | convolution fusion | flops 1132683264 | bytes 7323648 | tf_op jit(solution)/shard_map/dot_general | solution.py:73
  106.6 0.0 copy-start.11
  106.6 5.1 %collective-permute-start.2 = (bf16[1152,192]{0,1:T(8,128)(2,1)S(1)}, bf16[1152,192]{0,1:T(8,128)(2,1)}, u32[]{:S(2)}, u32[]{:S(2)}) collective-permute-start(bf16[1152,192]{0,1:T(8,128)(2,1)S(1)} %convolution_convert_fusion.4), channel_id=1, source_target_pairs={{0,1},{1,0},{2,3},{3,2},{4,5},{5,4},{6,7},{7,6},{8,9},{9,8},{10,11... | collective-permute-start | bytes 1327112 | tf_op jit(solution)/shard_map/ppermute | solution.py:47
  111.7 34.5 %all-gather.3.cloned.1.call-done = bf16[1152,2560]{1,0:T(8,128)(2,1)} async-done(((bf16[144,2560]{1,0:T(8,128)(2,1)}), bf16[1152,2560]{1,0:T(8,128)(2,1)}) %all-gather.3.cloned.1.call-update) | async-done | bytes 5898256 | tf_op jit(solution)/shard_map/all_gather | solution.py:41
  146.2 4.9 %convolution_convert_fusion.6 = bf16[1152,192]{0,1:T(8,128)(2,1)S(1)} fusion(bf16[1152,2560]{1,0:T(8,128)(2,1)} %all-gather.3.cloned.1.call-done, bf16[1,192,2560]{2,1,0:T(8,128)(2,1)S(1)} %copy-done.7), kind=kOutput, calls=%fused_computation.13 | convolution fusion | flops 1132683264 | bytes 7323648 | tf_op jit(solution)/shard_map/dot_general | solution.py:73
  151.1 1.4 collective-permute-start
  152.4 2.1 convolution_convert_fusion.5
  154.5 0.3 collective-permute-start.1
  154.8 7.9 %collective-permute-done = bf16[1152,192]{0,1:T(8,128)(2,1)S(1)} collective-permute-done((bf16[1152,192]{0,1:T(8,128)(2,1)S(1)}, bf16[1152,192]{0,1:T(8,128)(2,1)S(1)}, u32[]{:S(2)}, u32[]{:S(2)}) %collective-permute-start) | collective-permute-done | bytes 442400 | tf_op jit(solution)/shard_map/ppermute | solution.py:47
  162.7 9.5 %collective-permute-done.1 = bf16[1152,192]{0,1:T(8,128)(2,1)S(1)} collective-permute-done((bf16[1152,192]{0,1:T(8,128)(2,1)S(1)}, bf16[1152,192]{0,1:T(8,128)(2,1)S(1)}, u32[]{:S(2)}, u32[]{:S(2)}) %collective-permute-start.1) | collective-permute-done | bytes 442400 | tf_op jit(solution)/shard_map/ppermute | solution.py:47
  172.1 1.8 multiply_convert_fusion
  174.0 4.3 %convolution_convert_fusion = bf16[1152,2560]{1,0:T(8,128)(2,1)} fusion(bf16[1152,192]{0,1:T(8,128)(2,1)S(1)} %get-tuple-element.9, bf16[1,192,2560]{2,1,0:T(8,128)(2,1)S(1)} %copy-done), kind=kOutput, calls=%fused_computation.2 | convolution fusion | flops 1135411200 | bytes 7323648 | tf_op jit(solution)/shard_map/dot_general | solution.py:73
  178.3 0.0 reduce-scatter.5.cloned.1.call-update
  178.3 0.2 reduce-scatter.9.cloned.1.call-start
  178.6 0.9 copy-done.8
  179.5 1.7 fusion.6
  181.2 4.3 %fusion = bf16[1152,2560]{1,0:T(8,128)(2,1)} fusion(f32[1152,2560]{1,0:T(8,128)S(1)} %fusion.6, bf16[1152,192]{0,1:T(8,128)(2,1)S(1)} %get-tuple-element.7, bf16[1,192,2560]{2,1,0:T(8,128)(2,1)S(1)} %copy-done.10), kind=kOutput, calls=%fused_computation.1 | convolution fusion | flops 1138360320 | bytes 19120128 | tf_op jit(solution)/shard_map/dot_general | solution.py:73
  185.5 0.0 reduce-scatter.9.cloned.1.call-update
  185.5 36.0 %reduce-scatter.5.cloned.1.call-done = bf16[144,2560]{1,0:T(8,128)(2,1)} async-done(((bf16[1152,2560]{1,0:T(8,128)(2,1)}), bf16[144,2560]{1,0:T(8,128)(2,1)}) %reduce-scatter.5.cloned.1.call-update) | async-done | bytes 737296 | tf_op jit(solution)/shard_map/reduce_scatter | solution.py:51
  221.5 2.5 reshape.98
  224.0 9.3 %all-to-all-start.1 = ((bf16[16,9,2560]{2,1,0:T(8,128)(2,1)}), bf16[16,9,2560]{2,1,0:T(8,128)(2,1)}, u32[]{:S(2)}, u32[]{:S(2)}) async-start(bf16[16,9,2560]{2,1,0:T(8,128)(2,1)} %reshape.98), calls=%async_computation.2 | async-start | bytes 2621440 | tf_op jit(solution)/shard_map/all_to_all | solution.py:54
  233.3 34.4 %reduce-scatter.9.cloned.1.call-done = bf16[144,2560]{1,0:T(8,128)(2,1)} async-done(((bf16[1152,2560]{1,0:T(8,128)(2,1)}), bf16[144,2560]{1,0:T(8,128)(2,1)}) %reduce-scatter.9.cloned.1.call-update) | async-done | bytes 737296 | tf_op jit(solution)/shard_map/reduce_scatter | solution.py:51
  267.7 2.5 reshape.102
  270.2 9.3 %all-to-all-start.3 = ((bf16[16,9,2560]{2,1,0:T(8,128)(2,1)}), bf16[16,9,2560]{2,1,0:T(8,128)(2,1)S(1)}, u32[]{:S(2)}, u32[]{:S(2)}) async-start(bf16[16,9,2560]{2,1,0:T(8,128)(2,1)} %reshape.102), calls=%async_computation.6 | async-start | bytes 2621440 | tf_op jit(solution)/shard_map/all_to_all | solution.py:54
  279.5 0.0 reduce-scatter.7.cloned.1.call-start
  279.6 1.6 reshape.99
  281.2 1.2 convolution_convert_fusion.3
  282.4 0.0 reduce-scatter.7.cloned.1.call-update
  282.4 0.0 reduce-scatter.11.cloned.1.call-start
  282.5 29.5 %all-to-all-done.3 = bf16[16,9,2560]{2,1,0:T(8,128)(2,1)S(1)} async-done(((bf16[16,9,2560]{2,1,0:T(8,128)(2,1)}), bf16[16,9,2560]{2,1,0:T(8,128)(2,1)S(1)}, u32[]{:S(2)}, u32[]{:S(2)}) %all-to-all-start.3) | async-done | bytes 737312 | tf_op jit(solution)/shard_map/all_to_all | solution.py:54
  312.0 0.3 reshape.103
  312.3 1.2 convolution_convert_fusion.2
  313.5 0.0 reduce-scatter.11.cloned.1.call-update
  313.6 5.6 %convolution_bitcast_fusion = f32[1,192,2560]{2,1,0:T(8,128)} fusion(bf16[1152,192]{0,1:T(8,128)(2,1)S(1)} %get-tuple-element.9, bf16[1152,2560]{1,0:T(8,128)(2,1)} %all-gather.5.cloned.1.call-done), kind=kOutput, calls=%fused_computation.3 | convolution fusion | flops 1132462080 | bytes 8306688 | tf_op jit(solution)/shard_map/dot_general | solution.py:73
  319.2 2.7 convolution_bitcast_fusion.1
  321.9 2.7 convolution_bitcast_fusion.2
  324.6 17.2 %all_gather.13 = bf16[128,2560]{1,0:T(8,128)(2,1)S(1)} all-gather(bf16[16,2560]{1,0:T(8,128)(2,1)} %reduce-scatter.7.cloned.1.call-done), channel_id=1, replica_groups=mesh['dp'=16,'expert'=8,'tensor'=2] {'expert'}, dimensions={0}, use_global_device_ids=true | all-gather | bytes 737280 | tf_op jit(solution)/shard_map/all_gather | solution.py:63
  341.8 10.3 %reduce-scatter.11.cloned.1.call-done = bf16[16,2560]{1,0:T(8,128)(2,1)} async-done(((bf16[128,2560]{1,0:T(8,128)(2,1)}), bf16[16,2560]{1,0:T(8,128)(2,1)}) %reduce-scatter.11.cloned.1.call-update) | async-done | bytes 81936 | tf_op jit(solution)/shard_map/reduce_scatter | solution.py:60
  352.1 16.1 %all_gather.15 = bf16[128,2560]{1,0:T(8,128)(2,1)S(1)} all-gather(bf16[16,2560]{1,0:T(8,128)(2,1)} %reduce-scatter.11.cloned.1.call-done), channel_id=1, replica_groups=mesh['dp'=16,'expert'=8,'tensor'=2] {'expert'}, dimensions={0}, use_global_device_ids=true | all-gather | bytes 737280 | tf_op jit(solution)/shard_map/all_gather | solution.py:63
  368.3 0.8 copy.18
  369.1 0.8 copy.19
  (30 shorter events, 0.1 us)
Async XLA Ops:
  7.2 94.7 %copy-start = (bf16[1,192,2560]{2,1,0:T(8,128)(2,1)S(1)}, bf16[1,192,2560]{2,1,0:T(8,128)(2,1)}, u32[]{:S(2)}) copy-start(bf16[1,192,2560]{2,1,0:T(8,128)(2,1)} %param.12) | copy-start | bytes 2949124
  7.2 94.7 %all-gather.5.cloned.1.call-start = ((), (), s32[]{:S(2)}) async-start(), calls=%async_computation.11 | async-start | bytes 6635520 | tf_op jit(solution)/shard_map/all_gather | solution.py:41
  61.8 84.4 %all-gather.3.cloned.1.call-start = ((), (), s32[]{:S(2)}) async-start(), calls=%async_computation.8 | async-start | bytes 6635520 | tf_op jit(solution)/shard_map/all_gather | solution.py:41
  99.1 47.1 %copy-start.7 = (bf16[1,192,2560]{2,1,0:T(8,128)(2,1)S(1)}, bf16[1,192,2560]{2,1,0:T(8,128)(2,1)}, u32[]{:S(2)}) copy-start(bf16[1,192,2560]{2,1,0:T(8,128)(2,1)} %param.10) | copy-start | bytes 2949124
  99.1 122.4 %reduce-scatter.5.cloned.1.call-start = ((), (), s32[]{:S(2)}) async-start(), calls=%async_computation.9 | async-start | bytes 6635520 | tf_op jit(solution)/shard_map/reduce_scatter | solution.py:51
  106.6 47.9 %copy-start.11 = (bf16[1152,192]{0,1:T(8,128)(2,1)}, bf16[1152,192]{0,1:T(8,128)(2,1)S(1)}, u32[]{:S(2)}) copy-start(bf16[1152,192]{0,1:T(8,128)(2,1)S(1)} %convolution_convert_fusion.4) | copy-start | bytes 1327108
  106.6 45.8 %copy-start.9 = (bf16[1,192,2560]{2,1,0:T(8,128)(2,1)S(1)}, bf16[1,192,2560]{2,1,0:T(8,128)(2,1)}, u32[]{:S(2)}) copy-start(bf16[1,192,2560]{2,1,0:T(8,128)(2,1)} %param.11) | copy-start | bytes 2949124
  106.6 48.2 %collective-permute-start.2 = (bf16[1152,192]{0,1:T(8,128)(2,1)S(1)}, bf16[1152,192]{0,1:T(8,128)(2,1)}, u32[]{:S(2)}, u32[]{:S(2)}) collective-permute-start(bf16[1152,192]{0,1:T(8,128)(2,1)S(1)} %convolution_convert_fusion.4), channel_id=1, source_target_pairs={{0,1},{1,0},{2,3},{3,2},{4,5},{5,4},{6,7},{7,6},{8,9},{9,8},{10,11... | collective-permute-start | bytes 1327112 | tf_op jit(solution)/shard_map/ppermute | solution.py:47
  146.2 6.3 %copy-start.2 = (bf16[1152,2560]{1,0:T(8,128)(2,1)S(1)}, bf16[1152,2560]{1,0:T(8,128)(2,1)}, u32[]{:S(2)}) copy-start(bf16[1152,2560]{1,0:T(8,128)(2,1)} %all-gather.3.cloned.1.call-done) | copy-start | bytes 17694724
  151.1 11.6 %collective-permute-start = (bf16[1152,192]{0,1:T(8,128)(2,1)S(1)}, bf16[1152,192]{0,1:T(8,128)(2,1)S(1)}, u32[]{:S(2)}, u32[]{:S(2)}) collective-permute-start(bf16[1152,192]{0,1:T(8,128)(2,1)S(1)} %convolution_convert_fusion.6), channel_id=1, source_target_pairs={{0,1},{1,0},{2,3},{3,2},{4,5},{5,4},{6,7},{7,6},{8,9},{9,8},{10,11... | collective-permute-start | bytes 1327112 | tf_op jit(solution)/shard_map/ppermute | solution.py:47
  154.5 17.6 %collective-permute-start.1 = (bf16[1152,192]{0,1:T(8,128)(2,1)S(1)}, bf16[1152,192]{0,1:T(8,128)(2,1)S(1)}, u32[]{:S(2)}, u32[]{:S(2)}) collective-permute-start(bf16[1152,192]{0,1:T(8,128)(2,1)S(1)} %convolution_convert_fusion.5), channel_id=1, source_target_pairs={{0,1},{1,0},{2,3},{3,2},{4,5},{5,4},{6,7},{7,6},{8,9},{9,8},{10,11... | collective-permute-start | bytes 1327112 | tf_op jit(solution)/shard_map/ppermute | solution.py:47
  174.0 4.6 %copy-start.3 = (bf16[1152,192]{0,1:T(8,128)(2,1)}, bf16[1152,192]{0,1:T(8,128)(2,1)S(1)}, u32[]{:S(2)}) copy-start(bf16[1152,192]{0,1:T(8,128)(2,1)S(1)} %get-tuple-element.8) | copy-start | bytes 1327108
  174.0 7.2 %copy-start.5 = (bf16[1152,192]{0,1:T(8,128)(2,1)}, bf16[1152,192]{0,1:T(8,128)(2,1)S(1)}, u32[]{:S(2)}) copy-start(bf16[1152,192]{0,1:T(8,128)(2,1)S(1)} %get-tuple-element.7) | copy-start | bytes 1327108
  178.3 1.2 copy-start.8
  178.3 89.4 %reduce-scatter.9.cloned.1.call-start = ((), (), s32[]{:S(2)}) async-start(), calls=%async_computation.12 | async-start | bytes 6635520 | tf_op jit(solution)/shard_map/reduce_scatter | solution.py:51
  179.5 1.8 copy-start.10
  224.0 46.2 %all-to-all-start.1 = ((bf16[16,9,2560]{2,1,0:T(8,128)(2,1)}), bf16[16,9,2560]{2,1,0:T(8,128)(2,1)}, u32[]{:S(2)}, u32[]{:S(2)}) async-start(bf16[16,9,2560]{2,1,0:T(8,128)(2,1)} %reshape.98), calls=%async_computation.2 | async-start | bytes 2621440 | tf_op jit(solution)/shard_map/all_to_all | solution.py:54
  270.2 41.8 %all-to-all-start.3 = ((bf16[16,9,2560]{2,1,0:T(8,128)(2,1)}), bf16[16,9,2560]{2,1,0:T(8,128)(2,1)S(1)}, u32[]{:S(2)}, u32[]{:S(2)}) async-start(bf16[16,9,2560]{2,1,0:T(8,128)(2,1)} %reshape.102), calls=%async_computation.6 | async-start | bytes 2621440 | tf_op jit(solution)/shard_map/all_to_all | solution.py:54
  279.5 45.1 %reduce-scatter.7.cloned.1.call-start = ((), (), s32[]{:S(2)}) async-start(), calls=%async_computation.10 | async-start | bytes 737280 | tf_op jit(solution)/shard_map/reduce_scatter | solution.py:60
  282.4 69.7 %reduce-scatter.11.cloned.1.call-start = ((), (), s32[]{:S(2)}) async-start(), calls=%async_computation.13 | async-start | bytes 737280 | tf_op jit(solution)/shard_map/reduce_scatter | solution.py:60
  312.3 6.8 %slice-start = ((s8[5898240]{0:T(1024)(128)(4,1)}), s8[1703936]{0:T(1024)(128)(4,1)S(1)}, s32[]{:S(2)}) async-start(s8[5898240]{0:T(1024)(128)(4,1)} %bitcast.64), calls=%async_computation.14 | async-start | bytes 3407872
  313.6 5.6 %slice-start.1 = ((s8[5898240]{0:T(1024)(128)(4,1)}), s8[4194304]{0:T(1024)(128)(4,1)S(1)}, s32[]{:S(2)}) async-start(s8[5898240]{0:T(1024)(128)(4,1)} %bitcast.64), calls=%async_computation.15 | async-start | bytes 8388608
  313.6 5.6 %copy-start.6 = (bf16[1152,192]{0,1:T(8,128)(2,1)S(1)}, bf16[1152,192]{0,1:T(8,128)(2,1)}, u32[]{:S(2)}) copy-start(bf16[1152,192]{0,1:T(8,128)(2,1)} %copy-done.5) | copy-start | bytes 1327108
  319.2 2.7 copy-start.4
  319.2 50.8 %copy-start.1 = (bf16[1,192,2560]{2,1,0:T(8,128)(2,1)S(1)}, bf16[1,192,2560]{2,1,0:T(8,128)(2,1)}, u32[]{:S(2)}) copy-start(bf16[1,192,2560]{2,1,0:T(8,128)(2,1)} %param.12) | copy-start | bytes 2949124
Sparse Core Ops, SparseCore 0:
  61.9 39.8 all-gather.4
  104.3 41.8 all-gather.2
  178.4 43.0 reduce-scatter.4
  224.1 43.5 reduce-scatter.8
  283.2 33.1 reduce-scatter.6
  319.3 32.7 reduce-scatter.10

commit v2 on v1

v2 whole, which is shorter than its diff:
```python
import functools

import jax
import jax.numpy as jnp
from jax import lax
from jax.experimental import pallas as pl
from jax.experimental.pallas import tpu as pltpu
from jax.sharding import PartitionSpec as P

MESH = pl.DeviceIdType.MESH
SIDE = 4


def partner(owner, member, j, sign):
    y, z = owner // SIDE, owner % SIDE
    dy = member % 2 + 2 * j
    dz = (member // 2 - dy + SIDE) % SIDE
    if sign < 0:
        dy, dz = SIDE - dy, SIDE - dz
    return (y + dy) % SIDE * SIDE + (z + dz) % SIDE


class Place:
    def __init__(self):
        self.d = lax.axis_index("dp")
        self.h = lax.axis_index("expert")
        self.x, self.c = self.h // 2, self.h % 2
        self.right = self.column((self.x + 1) % SIDE)
        self.left = self.column((self.x + SIDE - 1) % SIDE)
        self.sibling = {"expert": self.x * 2 + 1 - self.c}

    def column(self, x):
        return {"expert": x * 2 + self.c}

    def to(self, j):
        return {"dp": partner(self.d, self.h, j, 1)}

    def back(self, j):
        return {"dp": partner(self.d, self.h, j, -1)}


def remote(src, dst, send, recv, device):
    return pltpu.make_async_remote_copy(
        src_ref=src, dst_ref=dst, send_sem=send, recv_sem=recv, device_id=device, device_id_type=MESH
    )


def greet(devices):
    barrier = pltpu.get_barrier_semaphore()
    for device in devices:
        pl.semaphore_signal(barrier, inc=1, device_id=device, device_id_type=MESH)
    pl.semaphore_wait(barrier, len(devices))


def greet_routes(place, devices, forward):
    barrier = pltpu.get_barrier_semaphore()
    inward = place.back if forward else place.to
    for device in devices + [inward(1)]:
        pl.semaphore_signal(barrier, inc=1, device_id=device, device_id_type=MESH)

    @pl.when(place.h > 0)
    def _():
        pl.semaphore_signal(barrier, inc=1, device_id=inward(0), device_id_type=MESH)

    pl.semaphore_wait(barrier, len(devices) + 1 + jnp.minimum(place.h, 1))


def direct(place, j, src, dst, send, recv, device, act):
    if j == 1:
        copy = remote(src, dst, send, recv, device)
        copy.start() if act == "start" else copy.wait_send()
        return

    @pl.when(place.h > 0)
    def _():
        copy = remote(src, dst, send, recv, device)
        copy.start() if act == "start" else copy.wait_send()

    if act == "start":

        @pl.when(place.h == 0)
        def _():
            pltpu.make_async_copy(src, dst, recv).start()


def landed(ref, sem):
    pltpu.make_async_copy(ref, ref, sem).wait()


def dispatch_kernel(tok, cot, tok_rows, cot_rows, far_send, far_recv, ring_send, ring_recv, sib_send, sib_recv):
    place = Place()
    x, c = place.x, place.c
    greet_routes(place, [place.left, place.right, place.sibling], True)
    inputs, outputs = (tok, cot), (tok_rows, cot_rows)
    home = 2 * place.h
    for a in range(2):
        for j in range(2):
            direct(place, j, inputs[a].at[j], outputs[a].at[home + j], far_send.at[a, j], far_recv.at[a, j], place.to(j), "start")

    pending = []

    def ring(a, block, side, slot):
        ref = outputs[a].at[block]
        copy = remote(ref, ref, ring_send.at[a, side, slot], ring_recv.at[a, side, slot], place.right if side == 0 else place.left)
        copy.start()
        pending.append(copy)

    def share(a, block, slot):
        ref = outputs[a].at[block]
        copy = remote(ref, ref, sib_send.at[a, slot], sib_recv.at[a, slot], place.sibling)
        copy.start()
        pending.append(copy)

    def block_of(shift, j):
        return 2 * ((x + SIDE + shift) % SIDE * 2 + c) + j

    def own(a):
        for j in range(2):
            landed(outputs[a].at[home + j], far_recv.at[a, j])
            ring(a, home + j, 0, j)
            ring(a, home + j, 1, j)
            share(a, home + j, j)

    def near(a):
        for j in range(2):
            for side, shift in ((0, -1), (1, 1)):
                block = block_of(shift, j)
                landed(outputs[a].at[block], ring_recv.at[a, side, j])
                if side == j:
                    ring(a, block, side, 2)
                share(a, block, 2 + 2 * side + j)

    def far(a):
        for side in range(2):
            block = block_of(2, side)
            landed(outputs[a].at[block], ring_recv.at[a, side, 2])
            share(a, block, 6 + side)

    own(0)
    near(0)
    own(1)
    far(0)
    near(1)
    far(1)
    for a in range(2):
        for slot in range(8):
            landed(outputs[a].at[slot], sib_recv.at[a, slot])
        for j in range(2):
            direct(place, j, inputs[a].at[j], outputs[a].at[home + j], far_send.at[a, j], far_recv.at[a, j], place.to(j), "sent")
    for copy in pending:
        copy.wait_send()


def dispatch(tok, cot, rows, width):
    any_spec = pl.BlockSpec(memory_space=pl.ANY)
    full = jax.ShapeDtypeStruct((16, rows, width), jnp.bfloat16)
    dma = pltpu.SemaphoreType.DMA
    return pl.pallas_call(
        dispatch_kernel,
        out_shape=(full, full),
        in_specs=[any_spec] * 2,
        out_specs=(any_spec, any_spec),
        scratch_shapes=[dma((2, 2)), dma((2, 2)), dma((2, 2, 3)), dma((2, 2, 3)), dma((2, 8)), dma((2, 8))],
        compiler_params=pltpu.CompilerParams(collective_id=0, has_side_effects=True),
        name="dispatch",
    )(tok, cot)


def add_blocks(dst, refs, chunk=512):
    width = dst.shape[-1]

    def step(i, carry):
        cols = pl.ds(pl.multiple_of(i * chunk, chunk), chunk)
        total = refs[0][:, cols].astype(jnp.float32)
        for ref in refs[1:]:
            total = total + ref[:, cols].astype(jnp.float32)
        dst[:, cols] = total.astype(dst.dtype)
        return carry

    lax.fori_loop(0, width // chunk, step, 0)


def home_kernel(
    part0, part1, out0, out1, sib0, sib1, sum0, sum1, ring0, ring1, fin0, fin1,
    sib_send, sib_recv, ring_send, ring_recv, far_send, far_recv,
):
    place = Place()
    x, c = place.x, place.c
    greet_routes(place, [place.left, place.right, place.sibling], False)
    parts, outs, sibs, sums, rings, fins = (
        (part0, part1), (out0, out1), (sib0, sib1), (sum0, sum1), (ring0, ring1), (fin0, fin1)
    )
    pending = []
    order = (2, 1, 3, 0)

    def column(shift):
        return (x + shift) % SIDE

    for a in range(2):
        for shift in order:
            for j in range(2):
                slot = 2 * shift + j
                src = parts[a].at[2 * (column(shift) * 2 + 1 - c) + j]
                copy = remote(src, sibs[a].at[slot], sib_send.at[a, slot], sib_recv.at[a, slot], place.sibling)
                copy.start()
                pending.append(copy)

    def send(a, shift, j, side, slot):
        copy = remote(
            sums[a].at[2 * shift + j], rings[a].at[3 * side + slot], ring_send.at[a, side, slot],
            ring_recv.at[a, side, slot], place.right if side == 0 else place.left,
        )
        copy.start()
        pending.append(copy)

    def first(a):
        for shift in order:
            for j in range(2):
                slot = 2 * shift + j
                landed(sibs[a].at[slot], sib_recv.at[a, slot])
                add_blocks(sums[a].at[slot], [parts[a].at[2 * (column(shift) * 2 + c) + j], sibs[a].at[slot]])
                if shift == 2:
                    send(a, 2, j, j, 0)
                elif shift == 1 and j == 1:
                    send(a, 1, 1, 0, 2)
                elif shift == 3 and j == 0:
                    send(a, 3, 0, 1, 1)

    def second(a):
        for side, shift, j, slot in ((0, 1, 0, 1), (1, 3, 1, 2)):
            got = rings[a].at[3 * side]
            landed(got, ring_recv.at[a, side, 0])
            mine = sums[a].at[2 * shift + j]
            add_blocks(mine, [mine, got])
            send(a, shift, j, side, slot)

    def third(a):
        for j in range(2):
            for side in range(2):
                landed(rings[a].at[3 * side + 1 + j], ring_recv.at[a, side, 1 + j])
            add_blocks(fins[a].at[j], [sums[a].at[j], rings[a].at[1 + j], rings[a].at[4 + j]])
            direct(place, j, fins[a].at[j], outs[a].at[j], far_send.at[a, j], far_recv.at[a, j], place.back(j), "start")

    first(0)
    second(0)
    first(1)
    third(0)
    second(1)
    third(1)
    for a in range(2):
        for j in range(2):
            landed(outs[a].at[j], far_recv.at[a, j])
            direct(place, j, fins[a].at[j], outs[a].at[j], far_send.at[a, j], far_recv.at[a, j], place.back(j), "sent")
    for copy in pending:
        copy.wait_send()


def bring_home(part0, part1):
    _, rows, width = part0.shape
    vmem = pl.BlockSpec(memory_space=pltpu.VMEM)

    def blocks(n):
        return jax.ShapeDtypeStruct((n, rows, width), jnp.bfloat16)

    shapes = [blocks(n) for n in (2, 2, 8, 8, 8, 8, 6, 6, 2, 2)]
    dma = pltpu.SemaphoreType.DMA
    return pl.pallas_call(
        home_kernel,
        out_shape=shapes,
        in_specs=[vmem] * 2,
        out_specs=[vmem] * len(shapes),
        scratch_shapes=[dma((2, 8)), dma((2, 8)), dma((2, 2, 3)), dma((2, 2, 3)), dma((2, 2)), dma((2, 2))],
        compiler_params=pltpu.CompilerParams(
            collective_id=1, has_side_effects=True, vmem_limit_bytes=56 * 1024 * 1024
        ),
        name="bring_home",
    )(part0, part1)[:2]


def tail_kernel(part, out, sib, half, got, sib_send, sib_recv, ring_send, ring_recv, all_send, all_recv, back_send, back_recv):
    place = Place()
    x, c = place.x, place.c
    rows = part.shape[1] // 8

    def column(shift):
        return (x + shift) % SIDE

    greet([place.column(column(k)) for k in (1, 2, 3)] + [place.sibling])
    pending = []

    def go(src, dst, send, recv, device):
        copy = remote(src, dst, send, recv, device)
        copy.start()
        pending.append(copy)

    def stripe(col, core):
        return pl.ds(pl.multiple_of((core * SIDE + col) * rows, rows), rows)

    for k in (2, 1, 3, 0):
        go(part.at[:, stripe(column(k), 1 - c)], sib.at[k], sib_send.at[k], sib_recv.at[k], place.sibling)
    for k in (2, 1, 3, 0):
        landed(sib.at[k], sib_recv.at[k])
        for a in range(2):
            add_blocks(half.at[k, a], [part.at[a, stripe(column(k), c)], sib.at[k, a]])
        if k:
            go(half.at[k], got.at[k - 1], ring_send.at[k - 1], ring_recv.at[k - 1], place.column(column(k)))
    for k in range(3):
        landed(got.at[k], ring_recv.at[k])
    mine = out.at[:, stripe(x, c)]
    for a in range(2):
        add_blocks(out.at[a, stripe(x, c)], [half.at[0, a]] + [got.at[k, a] for k in range(3)])
    for k in (2, 1, 3):
        go(mine, mine, all_send.at[k - 1], all_recv.at[k - 1], place.column(column(k)))
    go(mine, mine, back_send.at[0], back_recv.at[0], place.sibling)
    for k in (1, 3, 2):
        ref = out.at[:, stripe(column(SIDE - k), c)]
        landed(ref, all_recv.at[k - 1])
        go(ref, ref, back_send.at[k], back_recv.at[k], place.sibling)
    for k in range(4):
        landed(mine, back_recv.at[k])
    for copy in pending:
        copy.wait_send()


def tail_sum(part):
    _, tokens, width = part.shape
    vmem = pl.BlockSpec(memory_space=pltpu.VMEM)
    rows = tokens // 8

    def shape(*dims):
        return jax.ShapeDtypeStruct(dims, jnp.bfloat16)

    shapes = [shape(2, tokens, width), shape(4, 2, rows, width), shape(4, 2, rows, width), shape(3, 2, rows, width)]
    dma = pltpu.SemaphoreType.DMA
    return pl.pallas_call(
        tail_kernel,
        out_shape=shapes,
        in_specs=[vmem],
        out_specs=[vmem] * len(shapes),
        scratch_shapes=[dma((4,)), dma((4,)), dma((3,)), dma((3,)), dma((3,)), dma((3,)), dma((4,)), dma((4,))],
        compiler_params=pltpu.CompilerParams(collective_id=2, has_side_effects=True),
        name="tail_sum",
    )(part)[0]


def body(tokens, routes, route_weights, gate_weight, up_weight, down_weight, cotangent):
    experts = lax.axis_size("dp")
    gate_weight, up_weight, down_weight = gate_weight[0], up_weight[0], down_weight[0]
    hidden_share, half_width = gate_weight.shape
    tok_rows, top_count = routes.shape
    capacity = min(tok_rows, 3 * tok_rows * top_count // (2 * experts))
    own_rows = 2 * capacity
    pair_count = tok_rows * top_count

    flat_route = routes.T.reshape(pair_count)
    onehot = (flat_route[:, None] == jnp.arange(experts, dtype=jnp.int32)[None, :])
    running = jnp.cumsum(onehot.astype(jnp.int32), axis=0) - 1
    position = jnp.sum(jnp.where(onehot, running, 0), axis=1)
    target = flat_route * capacity + position
    owner, member = lax.axis_index("dp"), lax.axis_index("expert")
    own_index = jnp.arange(own_rows, dtype=jnp.int32)
    own_expert = jnp.where(
        own_index < capacity, partner(owner, member, 0, 1), partner(owner, member, 1, 1)
    )
    own_slot = own_expert * capacity + own_index % capacity
    selector = (own_slot[:, None] == target[None, :]).reshape(own_rows, top_count, tok_rows)
    weight_grid = jnp.sum(
        jnp.where(selector, route_weights.T[None], jnp.float32(0.0)), axis=1
    )
    own_weight = jnp.sum(weight_grid, axis=1, keepdims=True)
    own_place = jnp.any(selector, axis=1).astype(jnp.bfloat16)

    def select(values):
        return jnp.dot(own_place, values, preferred_element_type=jnp.float32)

    def blocks(values):
        return values.astype(jnp.bfloat16).reshape(-1, capacity, half_width)

    def width_sum(partial_values):
        mine = partial_values.astype(jnp.bfloat16)
        other = lax.ppermute(mine, "tensor", [(0, 1), (1, 0)])
        return mine.astype(jnp.float32) + other.astype(jnp.float32)

    rows, grad_rows = dispatch(
        blocks(select(tokens)), blocks(select(cotangent) * own_weight), capacity, half_width
    )
    rows = rows.reshape(experts * capacity, half_width)
    grad_rows = grad_rows.reshape(experts * capacity, half_width)

    nt = (((1,), (1,)), ((), ()))
    nn = (((1,), (0,)), ((), ()))
    tn = (((0,), (0,)), ((), ()))

    def mm(a, b, dims):
        return lax.dot_general(a, b, dims, preferred_element_type=jnp.float32)

    gate_val = width_sum(mm(rows, gate_weight, nt))
    up_val = width_sum(mm(rows, up_weight, nt))
    hidden_grad = width_sum(mm(grad_rows, down_weight, nt))
    sigmoid_gate = jax.nn.sigmoid(gate_val)
    activated = gate_val * sigmoid_gate
    hidden = (activated * up_val).astype(jnp.bfloat16)
    gate_delta = (
        hidden_grad * up_val * sigmoid_gate * (1.0 + gate_val * (1.0 - sigmoid_gate))
    ).astype(jnp.bfloat16)
    up_delta = (hidden_grad * activated).astype(jnp.bfloat16)
    down_part = mm(hidden, down_weight, nn)
    input_part = mm(gate_delta, gate_weight, nn) + mm(up_delta, up_weight, nn)
    expert_out, row_grad = bring_home(blocks(down_part), blocks(input_part))
    out_part = mm(weight_grid.astype(jnp.bfloat16), expert_out.reshape(own_rows, half_width), tn)
    grad_part = mm(own_place, row_grad.reshape(own_rows, half_width), tn)
    both = tail_sum(jnp.stack((out_part, grad_part)).astype(jnp.bfloat16))
    gate_grad = mm(gate_delta, rows, tn)
    up_grad = mm(up_delta, rows, tn)
    down_grad = mm(hidden, grad_rows, tn)
    return (both[0], both[1], gate_grad[None], up_grad[None], down_grad[None])


def solution(mesh):
    in_specs = (
        P("dp", "tensor"),
        P("dp", None),
        P("dp", None),
        P("dp", "expert", "tensor"),
        P("dp", "expert", "tensor"),
        P("dp", "expert", "tensor"),
        P("dp", "tensor"),
    )
    out_specs = (
        P("dp", "tensor"),
        P("dp", "tensor"),
        P("dp", "expert", "tensor"),
        P("dp", "expert", "tensor"),
        P("dp", "expert", "tensor"),
    )
    return jax.shard_map(body, mesh=mesh, in_specs=in_specs, out_specs=out_specs, check_vma=False)
```

time: 378 us -> 273 us (0.72)
  Pallas kernels: 0 us -> 200 us
  waiting for transfers between devices: 165 us -> 23.5 us
  blocking collectives: 111 us -> 0 us
  starting transfers between devices: 25.7 us -> 3.08 us
  between operations: 14.4 us -> 0.91 us
  local copies, waits for them, and re-layouts: 15.4 us -> 2.72 us
    pallas_call x0 -> x3, Pallas kernels: none -> 200 us  [the longest x1 84.6 us: bring_home(): pl.pallas_call(home_kernel, out_shape=shapes, in_specs=[vmem] * 2, out_sp...]
    reduce_scatter x4 -> x0, waiting for transfers between devices: 80.7 us -> none  [the longest x2 70.4 us: home(): lax.psum_scatter(partial_rows.astype(jnp.bfloat16), 'expert', scatter_dim...]
    all_to_all x2 -> x0, blocking collectives: 78 us -> none  [dispatch(): lax.all_to_all(rows.reshape(dp_count, share_rows, half_width), 'dp', spli...]
    all_gather x2 -> x0, waiting for transfers between devices: 37.2 us -> none  [dispatch(): lax.all_gather(arrived.reshape(own_rows, half_width), 'expert', axis=0, t...]
    all_gather x2 -> x0, blocking collectives: 33.3 us -> none  [token_sum(): return lax.all_gather(part, 'expert', axis=0, tiled=True)]
    all_to_all x2 -> x0, waiting for transfers between devices: 29.5 us -> none  [home(): lax.all_to_all(summed.reshape(dp_count, share_rows, half_width), 'dp', sp...]
    all_to_all x2 -> x0, starting transfers between devices: 18.6 us -> none  [home(): lax.all_to_all(summed.reshape(dp_count, share_rows, half_width), 'dp', sp...]
    reshape x8 -> x0, local copies, waits for them, and re-layouts: 12.5 us -> none  [the longest x2 4.99 us: dispatch(): arrived.reshape(own_rows, half_width)]
  transfers between devices with their start and end apart: 11 -> 3, of which waited for: 8 -> 3; matrix products, arithmetic and copies ran while one was open for 11% -> 2% of each run, Pallas kernels for 0% -> 0%
where the time goes in v2:
time: 273 us; the launch traced here: 272 us
  Pallas kernels  200 us (73%)
  matrix products  35.4 us (13%)
  waiting for transfers between devices  23.5 us (9%)
  other arithmetic  6.87 us (3%)
  starting transfers between devices  3.08 us (1%)
    pallas_call x1, Pallas kernels, bring_home(): pl.pallas_call(home_kernel, out_shape=shapes, in_specs=[vmem] * 2, out_sp...  84.6 us
    pallas_call x1, Pallas kernels, dispatch(): pl.pallas_call(dispatch_kernel, out_shape=(full, full), in_specs=[any_spe...  82.7 us
    pallas_call x1, Pallas kernels, tail_sum(): pl.pallas_call(tail_kernel, out_shape=shapes, in_specs=[vmem], out_specs=...  32.2 us
    dot_general x11, matrix products, mm(): return lax.dot_general(a, b, dims, preferred_element_type=jnp.float32)  30.8 us
    ppermute x3, waiting for transfers between devices, width_sum(): other = lax.ppermute(mine, 'tensor', [(0, 1), (1, 0)])  23.5 us
  transfers between devices with their start and end apart: 3, of which 3 were waited for; matrix products, arithmetic and copies ran while one was open for 2% of the time, Pallas kernels for 0%

profile of v2, /device:TPU:1, one launch (start us, length us, event | category | flops | bytes accessed | tf_op | source)
XLA Modules:
  0.0 272.1 jit_solution(7522352780956301244)
XLA Ops:
  0.6 0.0 copy-start
  0.8 0.8 fusion.14
  1.5 1.7 reduce-window.6
  3.2 0.3 slice_reduce_fusion
  3.5 0.8 fusion.13
  4.3 0.7 bitcast_add_fusion
  5.0 0.1 compare_reduce_fusion
  5.1 0.9 select_reduce_fusion.1
  6.0 2.3 convolution_convert_fusion.1
  8.3 2.3 fusion.1
  10.6 82.7 %dispatch.1 = (bf16[16,72,2560]{2,1,0:T(8,128)(2,1)}, bf16[16,72,2560]{2,1,0:T(8,128)(2,1)}) custom-call(bf16[2,72,2560]{2,1,0:T(8,128)(2,1)} %bitcast.93, bf16[2,72,2560]{2,1,0:T(8,128)(2,1)} %bitcast.92), custom_call_target="tpu_custom_call" | custom-call | tf_op jit(solution)/shard_map/dispatch/pallas_call | solution.py:158
  93.4 0.0 slice-start
  93.4 0.0 copy-start.3
  93.4 0.0 slice-start.1
  93.4 0.0 slice-start.2
  93.4 5.1 %convolution_convert_fusion.6 = bf16[1152,192]{0,1:T(8,128)(2,1)S(1)} fusion(bf16[1152,2560]{1,0:T(8,128)(2,1)} %bitcast.80, bf16[1,192,2560]{2,1,0:T(8,128)(2,1)} %param.10), kind=kOutput, calls=%fused_computation.15 | convolution fusion | flops 1132683264 | bytes 7323648 | tf_op jit(solution)/shard_map/dot_general | solution.py:395
  98.6 0.0 slice-start.3
  98.6 1.3 collective-permute-start
  99.8 0.0 slice-done
  99.8 0.0 copy-done.3
  99.8 0.0 slice-done.1
  99.8 2.1 convolution_convert_fusion.5
  101.9 0.4 collective-permute-start.1
  102.3 0.0 copy-done
  102.3 0.0 slice-done.2
  102.3 0.0 slice-done.3
  102.3 2.1 convolution_convert_fusion.4
  104.4 1.4 collective-permute-start.2
  105.8 4.6 %collective-permute-done = bf16[1152,192]{0,1:T(8,128)(2,1)S(1)} collective-permute-done((bf16[1152,192]{0,1:T(8,128)(2,1)S(1)}, bf16[1152,192]{0,1:T(8,128)(2,1)S(1)}, u32[]{:S(2)}, u32[]{:S(2)}) %collective-permute-start) | collective-permute-done | bytes 442400 | tf_op jit(solution)/shard_map/ppermute | solution.py:381
  110.4 9.5 %collective-permute-done.1 = bf16[1152,192]{0,1:T(8,128)(2,1)S(1)} collective-permute-done((bf16[1152,192]{0,1:T(8,128)(2,1)S(1)}, bf16[1152,192]{0,1:T(8,128)(2,1)S(1)}, u32[]{:S(2)}, u32[]{:S(2)}) %collective-permute-start.1) | collective-permute-done | bytes 442400 | tf_op jit(solution)/shard_map/ppermute | solution.py:381
  119.9 9.5 %collective-permute-done.2 = bf16[1152,192]{0,1:T(8,128)(2,1)S(1)} collective-permute-done((bf16[1152,192]{0,1:T(8,128)(2,1)S(1)}, bf16[1152,192]{0,1:T(8,128)(2,1)S(1)}, u32[]{:S(2)}, u32[]{:S(2)}) %collective-permute-start.2) | collective-permute-done | bytes 442400 | tf_op jit(solution)/shard_map/ppermute | solution.py:381
  129.3 0.7 multiply_convert_fusion
  130.0 2.8 %convolution_bitcast_fusion = f32[1,192,2560]{2,1,0:T(8,128)} fusion(bf16[1152,192]{0,1:T(8,128)(2,1)S(1)} %get-tuple-element.19, bf16[1152,2560]{1,0:T(8,128)(2,1)S(1)} %bitcast.91), kind=kOutput, calls=%fused_computation.3 | convolution fusion | flops 1132462080 | bytes 8306688 | tf_op jit(solution)/shard_map/dot_general | solution.py:395
  132.8 4.3 %convolution_convert_fusion = bf16[1152,2560]{1,0:T(8,128)(2,1)} fusion(bf16[1152,192]{0,1:T(8,128)(2,1)S(1)} %get-tuple-element.19, bf16[1,192,2560]{2,1,0:T(8,128)(2,1)S(1)} %copy-done), kind=kOutput, calls=%fused_computation.2 | convolution fusion | flops 1135411200 | bytes 7323648 | tf_op jit(solution)/shard_map/dot_general | solution.py:395
  137.1 0.0 copy-start.2
  137.1 2.7 convolution_bitcast_fusion.2
  139.8 0.0 copy-done.2
  139.8 1.7 fusion.8
  141.5 2.8 %convolution_bitcast_fusion.1 = f32[1,192,2560]{2,1,0:T(8,128)} fusion(bf16[1152,192]{0,1:T(8,128)(2,1)S(1)} %get-tuple-element.17, bf16[1152,2560]{1,0:T(8,128)(2,1)S(1)} %bitcast.85), kind=kOutput, calls=%fused_computation.4 | convolution fusion | flops 1132462080 | bytes 8306688 | tf_op jit(solution)/shard_map/dot_general | solution.py:395
  144.3 4.3 %fusion = bf16[1152,2560]{1,0:T(8,128)(2,1)} fusion(f32[1152,2560]{1,0:T(8,128)S(1)} %fusion.8, bf16[1152,192]{0,1:T(8,128)(2,1)S(1)} %get-tuple-element.17, bf16[1,192,2560]{2,1,0:T(8,128)(2,1)S(1)} %copy-done.3), kind=kOutput, calls=%fused_computation.1 | convolution fusion | flops 1138360320 | bytes 19120128 | tf_op jit(solution)/shard_map/dot_general | solution.py:395
  148.6 0.0 copy-start.1
  148.6 84.6 %bring_home.1 = (bf16[2,72,2560]{2,1,0:T(8,128)(2,1)}, bf16[2,72,2560]{2,1,0:T(8,128)(2,1)}, bf16[8,72,2560]{2,1,0:T(8,128)(2,1)}, bf16[8,72,2560]{2,1,0:T(8,128...) custom-call(bf16[16,72,2560]{2,1,0:T(8,128)(2,1)} %bitcast.86, ...), custom_call_target="tpu_custom_call" | custom-call | tf_op jit(solution)/shard_map/bring_home/pallas_call | solution.py:267
  233.3 1.5 fusion.2
  234.8 1.5 fusion.3
  236.3 1.2 pad_maximum_fusion.part
  237.4 32.2 %tail_sum.1 = (bf16[2,128,2560]{2,1,0:T(8,128)(2,1)}, bf16[4,2,16,2560]{3,2,1,0:T(8,128)(2,1)}, bf16[4,2,16,2560]{3,2,1,0:T(8,128)(2,1)}, bf16[3,2,16,2560]{3,2,1,0:T(8,128)(2,1)}) custom-call(bf16[2,128,2560]{2,1,0:T(8,128)(2,1)} %pad_maximum_fusion.part), custom_call_target="tpu_custom_call" | custom-call | tf_op jit(solution)/shard_map/tail_sum/pallas_call | solution.py:335
  269.7 2.4 slice_bitcast_fusion
  272.1 0.0 copy-done.1
  (4 shorter events, 0.0 us)
Async XLA Ops:
  0.6 101.7 %copy-start = (bf16[1,192,2560]{2,1,0:T(8,128)(2,1)S(1)}, bf16[1,192,2560]{2,1,0:T(8,128)(2,1)}, u32[]{:S(2)}) copy-start(bf16[1,192,2560]{2,1,0:T(8,128)(2,1)} %param.12) | copy-start | bytes 2949124
  93.4 6.5 %slice-start = ((s8[5898240]{0:T(1024)(128)(4,1)}), s8[4194304]{0:T(1024)(128)(4,1)S(1)}, s32[]{:S(2)}) async-start(s8[5898240]{0:T(1024)(128)(4,1)} %bitcast.81), calls=%async_computation | async-start | bytes 8388608
  93.4 6.5 %copy-start.3 = (bf16[1,192,2560]{2,1,0:T(8,128)(2,1)S(1)}, bf16[1,192,2560]{2,1,0:T(8,128)(2,1)}, u32[]{:S(2)}) copy-start(bf16[1,192,2560]{2,1,0:T(8,128)(2,1)} %param.11) | copy-start | bytes 2949124
  93.4 6.5 %slice-start.1 = ((s8[5898240]{0:T(1024)(128)(4,1)}), s8[1703936]{0:T(1024)(128)(4,1)S(1)}, s32[]{:S(2)}) async-start(s8[5898240]{0:T(1024)(128)(4,1)} %bitcast.81), calls=%async_computation.1 | async-start | bytes 3407872
  93.4 8.9 %slice-start.2 = ((s8[5898240]{0:T(1024)(128)(4,1)}), s8[4194304]{0:T(1024)(128)(4,1)S(1)}, s32[]{:S(2)}) async-start(s8[5898240]{0:T(1024)(128)(4,1)} %bitcast.88), calls=%async_computation.2 | async-start | bytes 8388608
  98.6 3.8 %slice-start.3 = ((s8[5898240]{0:T(1024)(128)(4,1)}), s8[1703936]{0:T(1024)(128)(4,1)S(1)}, s32[]{:S(2)}) async-start(s8[5898240]{0:T(1024)(128)(4,1)} %bitcast.88), calls=%async_computation.3 | async-start | bytes 3407872
  98.6 11.8 %collective-permute-start = (bf16[1152,192]{0,1:T(8,128)(2,1)S(1)}, bf16[1152,192]{0,1:T(8,128)(2,1)S(1)}, u32[]{:S(2)}, u32[]{:S(2)}) collective-permute-start(bf16[1152,192]{0,1:T(8,128)(2,1)S(1)} %convolution_convert_fusion.6), channel_id=1, source_target_pairs={{0,1},{1,0},{2,3},{3,2},{4,5},{5,4},{6,7},{7,6},{8,9},{9,8},{10,11... | collective-permute-start | bytes 1327112 | tf_op jit(solution)/shard_map/ppermute | solution.py:381
  101.9 17.9 %collective-permute-start.1 = (bf16[1152,192]{0,1:T(8,128)(2,1)S(1)}, bf16[1152,192]{0,1:T(8,128)(2,1)S(1)}, u32[]{:S(2)}, u32[]{:S(2)}) collective-permute-start(bf16[1152,192]{0,1:T(8,128)(2,1)S(1)} %convolution_convert_fusion.5), channel_id=1, source_target_pairs={{0,1},{1,0},{2,3},{3,2},{4,5},{5,4},{6,7},{7,6},{8,9},{9,8},{10,11... | collective-permute-start | bytes 1327112 | tf_op jit(solution)/shard_map/ppermute | solution.py:381
  104.4 24.9 %collective-permute-start.2 = (bf16[1152,192]{0,1:T(8,128)(2,1)S(1)}, bf16[1152,192]{0,1:T(8,128)(2,1)S(1)}, u32[]{:S(2)}, u32[]{:S(2)}) collective-permute-start(bf16[1152,192]{0,1:T(8,128)(2,1)S(1)} %convolution_convert_fusion.4), channel_id=1, source_target_pairs={{0,1},{1,0},{2,3},{3,2},{4,5},{5,4},{6,7},{7,6},{8,9},{9,8},{10,11... | collective-permute-start | bytes 1327112 | tf_op jit(solution)/shard_map/ppermute | solution.py:381
  137.1 2.7 copy-start.2
  148.6 123.5 %copy-start.1 = (bf16[1,192,2560]{2,1,0:T(8,128)(2,1)S(1)}, bf16[1,192,2560]{2,1,0:T(8,128)(2,1)}, u32[]{:S(2)}) copy-start(bf16[1,192,2560]{2,1,0:T(8,128)(2,1)} %param.12) | copy-start | bytes 2949124

commit v3 on v2

--- a/solution.py
+++ b/solution.py
@@ -181,11 +181,33 @@
 
 
 def home_kernel(
-    part0, part1, out0, out1, sib0, sib1, sum0, sum1, ring0, ring1, fin0, fin1,
-    sib_send, sib_recv, ring_send, ring_recv, far_send, far_recv,
+    part0, part1, left0, left1, left2, rows, grad_rows,
+    out0, out1, sib0, sib1, sum0, sum1, ring0, ring1, fin0, fin1, grad0, grad1, grad2,
+    sib_send, sib_recv, ring_send, ring_recv, far_send, far_recv, right_rows, weight_sum, load_sem, store_sem,
 ):
     place = Place()
     x, c = place.x, place.c
+    lefts, grads = (left0, left1, left2), (grad0, grad1, grad2)
+    loads = [pltpu.make_async_copy(src, right_rows, load_sem) for src in (rows, grad_rows)]
+    stores = [pltpu.make_async_copy(weight_sum.at[i], grads[i], store_sem.at[i]) for i in range(3)]
+    loads[0].start()
+
+    def weight_grad(i, chunk=512):
+        if i != 1:
+            loads[i // 2].wait()
+
+        def step(k, carry):
+            cols = pl.ds(pl.multiple_of(k * chunk, chunk), chunk)
+            weight_sum[i, :, cols] = jnp.dot(
+                lefts[i][...], right_rows[:, cols], preferred_element_type=jnp.float32
+            )
+            return carry
+
+        lax.fori_loop(0, right_rows.shape[1] // chunk, step, 0)
+        stores[i].start()
+        if i == 1:
+            loads[1].start()
+
     greet_routes(place, [place.left, place.right, place.sibling], False)
     parts, outs, sibs, sums, rings, fins = (
         (part0, part1), (out0, out1), (sib0, sib1), (sum0, sum1), (ring0, ring1), (fin0, fin1)
@@ -242,10 +264,13 @@
             direct(place, j, fins[a].at[j], outs[a].at[j], far_send.at[a, j], far_recv.at[a, j], place.back(j), "start")
 
     first(0)
+    weight_grad(0)
     second(0)
     first(1)
+    weight_grad(1)
     third(0)
     second(1)
+    weight_grad(2)
     third(1)
     for a in range(2):
         for j in range(2):
@@ -253,10 +278,14 @@
             direct(place, j, fins[a].at[j], outs[a].at[j], far_send.at[a, j], far_recv.at[a, j], place.back(j), "sent")
     for copy in pending:
         copy.wait_send()
-
-
-def bring_home(part0, part1):
+    for copy in stores:
+        copy.wait()
+
+
+def bring_home(part0, part1, lefts, token_rows, grad_rows):
     _, rows, width = part0.shape
+    share, slots = lefts[0].shape
+    any_spec = pl.BlockSpec(memory_space=pl.ANY)
     vmem = pl.BlockSpec(memory_space=pltpu.VMEM)
 
     def blocks(n):
@@ -264,23 +293,32 @@
 
     shapes = [blocks(n) for n in (2, 2, 8, 8, 8, 8, 6, 6, 2, 2)]
     dma = pltpu.SemaphoreType.DMA
-    return pl.pallas_call(
+    grad_shapes = [jax.ShapeDtypeStruct((share, width), jnp.float32)] * 3
+    results = pl.pallas_call(
         home_kernel,
-        out_shape=shapes,
-        in_specs=[vmem] * 2,
-        out_specs=[vmem] * len(shapes),
-        scratch_shapes=[dma((2, 8)), dma((2, 8)), dma((2, 2, 3)), dma((2, 2, 3)), dma((2, 2)), dma((2, 2))],
+        out_shape=shapes + grad_shapes,
+        in_specs=[vmem] * 5 + [any_spec] * 2,
+        out_specs=[vmem] * len(shapes) + [any_spec] * 3,
+        scratch_shapes=[
+            dma((2, 8)), dma((2, 8)), dma((2, 2, 3)), dma((2, 2, 3)), dma((2, 2)), dma((2, 2)),
+            pltpu.VMEM((slots, width), jnp.bfloat16), pltpu.VMEM((3, share, width), jnp.float32), dma, dma((3,)),
+        ],
         compiler_params=pltpu.CompilerParams(
-            collective_id=1, has_side_effects=True, vmem_limit_bytes=56 * 1024 * 1024
+            collective_id=1, has_side_effects=True, vmem_limit_bytes=58 * 1024 * 1024
         ),
         name="bring_home",
-    )(part0, part1)[:2]
-
-
-def tail_kernel(part, out, sib, half, got, sib_send, sib_recv, ring_send, ring_recv, all_send, all_recv, back_send, back_recv):
+    )(part0, part1, *lefts, token_rows, grad_rows)
+    return results[:2], results[-3:]
+
+
+def tail_kernel(
+    part0, part1, out0, out1, sib, half, got,
+    sib_send, sib_recv, ring_send, ring_recv, all_send, all_recv, back_send, back_recv,
+):
     place = Place()
     x, c = place.x, place.c
-    rows = part.shape[1] // 8
+    parts, outs = (part0, part1), (out0, out1)
+    rows = part0.shape[0] // 8
 
     def column(shift):
         return (x + shift) % SIDE
@@ -297,50 +335,54 @@
         return pl.ds(pl.multiple_of((core * SIDE + col) * rows, rows), rows)
 
     for k in (2, 1, 3, 0):
-        go(part.at[:, stripe(column(k), 1 - c)], sib.at[k], sib_send.at[k], sib_recv.at[k], place.sibling)
+        for a in range(2):
+            src = parts[a].at[stripe(column(k), 1 - c)]
+            go(src, sib.at[k, a], sib_send.at[a, k], sib_recv.at[a, k], place.sibling)
     for k in (2, 1, 3, 0):
-        landed(sib.at[k], sib_recv.at[k])
         for a in range(2):
-            add_blocks(half.at[k, a], [part.at[a, stripe(column(k), c)], sib.at[k, a]])
+            landed(sib.at[k, a], sib_recv.at[a, k])
+            add_blocks(half.at[k, a], [parts[a].at[stripe(column(k), c)], sib.at[k, a]])
         if k:
             go(half.at[k], got.at[k - 1], ring_send.at[k - 1], ring_recv.at[k - 1], place.column(column(k)))
     for k in range(3):
         landed(got.at[k], ring_recv.at[k])
-    mine = out.at[:, stripe(x, c)]
-    for a in range(2):
-        add_blocks(out.at[a, stripe(x, c)], [half.at[0, a]] + [got.at[k, a] for k in range(3)])
-    for k in (2, 1, 3):
-        go(mine, mine, all_send.at[k - 1], all_recv.at[k - 1], place.column(column(k)))
-    go(mine, mine, back_send.at[0], back_recv.at[0], place.sibling)
-    for k in (1, 3, 2):
-        ref = out.at[:, stripe(column(SIDE - k), c)]
-        landed(ref, all_recv.at[k - 1])
-        go(ref, ref, back_send.at[k], back_recv.at[k], place.sibling)
-    for k in range(4):
-        landed(mine, back_recv.at[k])
+    mine = [out.at[stripe(x, c)] for out in outs]
+    for a in range(2):
+        add_blocks(mine[a], [half.at[0, a]] + [got.at[k, a] for k in range(3)])
+        for k in (2, 1, 3):
+            go(mine[a], mine[a], all_send.at[a, k - 1], all_recv.at[a, k - 1], place.column(column(k)))
+        go(mine[a], mine[a], back_send.at[a, 0], back_recv.at[a, 0], place.sibling)
+    for a in range(2):
+        for k in (1, 3, 2):
+            ref = outs[a].at[stripe(column(SIDE - k), c)]
+            landed(ref, all_recv.at[a, k - 1])
+            go(ref, ref, back_send.at[a, k], back_recv.at[a, k], place.sibling)
+    for a in range(2):
+        for k in range(4):
+            landed(mine[a], back_recv.at[a, k])
     for copy in pending:
         copy.wait_send()
 
 
-def tail_sum(part):
-    _, tokens, width = part.shape
+def tail_sum(part0, part1):
+    tokens, width = part0.shape
     vmem = pl.BlockSpec(memory_space=pltpu.VMEM)
     rows = tokens // 8
 
     def shape(*dims):
         return jax.ShapeDtypeStruct(dims, jnp.bfloat16)
 
-    shapes = [shape(2, tokens, width), shape(4, 2, rows, width), shape(4, 2, rows, width), shape(3, 2, rows, width)]
+    shapes = [shape(tokens, width), shape(tokens, width), shape(4, 2, rows, width), shape(4, 2, rows, width), shape(3, 2, rows, width)]
     dma = pltpu.SemaphoreType.DMA
     return pl.pallas_call(
         tail_kernel,
         out_shape=shapes,
-        in_specs=[vmem],
+        in_specs=[vmem] * 2,
         out_specs=[vmem] * len(shapes),
-        scratch_shapes=[dma((4,)), dma((4,)), dma((3,)), dma((3,)), dma((3,)), dma((3,)), dma((4,)), dma((4,))],
+        scratch_shapes=[dma((2, 4)), dma((2, 4)), dma((3,)), dma((3,)), dma((2, 3)), dma((2, 3)), dma((2, 4)), dma((2, 4))],
         compiler_params=pltpu.CompilerParams(collective_id=2, has_side_effects=True),
         name="tail_sum",
-    )(part)[0]
+    )(part0, part1)[:2]
 
 
 def body(tokens, routes, route_weights, gate_weight, up_weight, down_weight, cotangent):
@@ -406,13 +448,12 @@
     up_delta = (hidden_grad * activated).astype(jnp.bfloat16)
     down_part = mm(hidden, down_weight, nn)
     input_part = mm(gate_delta, gate_weight, nn) + mm(up_delta, up_weight, nn)
-    expert_out, row_grad = bring_home(blocks(down_part), blocks(input_part))
+    (expert_out, row_grad), (gate_grad, up_grad, down_grad) = bring_home(
+        blocks(down_part), blocks(input_part), (gate_delta.T, up_delta.T, hidden.T), rows, grad_rows
+    )
     out_part = mm(weight_grid.astype(jnp.bfloat16), expert_out.reshape(own_rows, half_width), tn)
     grad_part = mm(own_place, row_grad.reshape(own_rows, half_width), tn)
-    both = tail_sum(jnp.stack((out_part, grad_part)).astype(jnp.bfloat16))
-    gate_grad = mm(gate_delta, rows, tn)
-    up_grad = mm(up_delta, rows, tn)
-    down_grad = mm(hidden, grad_rows, tn)
+    both = tail_sum(out_part.astype(jnp.bfloat16), grad_part.astype(jnp.bfloat16))
     return (both[0], both[1], gate_grad[None], up_grad[None], down_grad[None])
 
 

time: 273 us -> 272 us (level)
  local copies, waits for them, and re-layouts: 2.72 us -> 9.97 us
  matrix products: 35.4 us -> 28.8 us
    unnamed x16 -> x31, local copies, waits for them, and re-layouts: 0.04 us -> 9.71 us
    dot_general x11 -> x8, matrix products: 30.8 us -> 24.2 us  [mm(): return lax.dot_general(a, b, dims, preferred_element_type=jnp.float32)]
where the time goes in v3:
time: 272 us
  Pallas kernels  200 us (74%)
  matrix products  28.8 us (11%)
  waiting for transfers between devices  23.5 us (9%)
  local copies, waits for them, and re-layouts  9.97 us (4%)
  other arithmetic  5.68 us (2%)
  starting transfers between devices  3.08 us (1%)
    pallas_call x1, Pallas kernels, bring_home(): pl.pallas_call(home_kernel, out_shape=shapes + grad_shapes, in_specs=[vme...  85.1 us
    pallas_call x1, Pallas kernels, dispatch(): pl.pallas_call(dispatch_kernel, out_shape=(full, full), in_specs=[any_spe...  82.7 us
    pallas_call x1, Pallas kernels, tail_sum(): pl.pallas_call(tail_kernel, out_shape=shapes, in_specs=[vmem] * 2, out_sp...  31.9 us
    dot_general x8, matrix products, mm(): return lax.dot_general(a, b, dims, preferred_element_type=jnp.float32)  24.2 us
    ppermute x3, waiting for transfers between devices, width_sum(): other = lax.ppermute(mine, 'tensor', [(0, 1), (1, 0)])  23.5 us
    unnamed x31, local copies, waits for them, and re-layouts  9.71 us
  transfers between devices with their start and end apart: 3, of which 3 were waited for; matrix products, arithmetic and copies ran while one was open for 2% of the time, Pallas kernels for 0%

profile of v3, /device:TPU:1, one launch (start us, length us, event | category | flops | bytes accessed | tf_op | source)
XLA Modules:
  0.0 271.8 jit_solution(5205214521029856272)
XLA Ops:
  0.6 0.0 copy-start
  0.8 0.8 fusion.12
  1.5 1.7 reduce-window.6
  3.2 0.3 slice_reduce_fusion
  3.5 0.8 fusion.11
  4.3 0.7 bitcast_add_fusion
  5.0 0.1 compare_reduce_fusion
  5.1 0.9 select_reduce_fusion.1
  6.0 2.3 convolution_convert_fusion.1
  8.3 2.3 fusion.1
  10.6 82.7 %dispatch.1 = (bf16[16,72,2560]{2,1,0:T(8,128)(2,1)}, bf16[16,72,2560]{2,1,0:T(8,128)(2,1)}) custom-call(bf16[2,72,2560]{2,1,0:T(8,128)(2,1)} %bitcast.81, bf16[2,72,2560]{2,1,0:T(8,128)(2,1)} %bitcast.80), custom_call_target="tpu_custom_call" | custom-call | tf_op jit(solution)/shard_map/dispatch/pallas_call | solution.py:158
  93.4 0.0 slice-start
  93.4 0.0 copy-start.8
  93.4 0.0 slice-start.1
  93.4 0.0 slice-start.2
  93.4 5.1 %convolution_convert_fusion.6 = bf16[1152,192]{0,1:T(8,128)(2,1)S(1)} fusion(bf16[1152,2560]{1,0:T(8,128)(2,1)} %bitcast.68, bf16[1,192,2560]{2,1,0:T(8,128)(2,1)} %param.10), kind=kOutput, calls=%fused_computation.10 | convolution fusion | flops 1132683264 | bytes 7323648 | tf_op jit(solution)/shard_map/dot_general | solution.py:437
  98.6 0.0 slice-start.3
  98.6 1.3 collective-permute-start
  99.8 0.0 slice-done
  99.8 0.0 copy-done.8
  99.8 0.0 slice-done.1
  99.8 2.1 convolution_convert_fusion.5
  101.9 0.4 collective-permute-start.1
  102.3 0.0 copy-done
  102.3 0.0 slice-done.2
  102.3 0.0 slice-done.3
  102.3 2.1 convolution_convert_fusion.4
  104.4 0.0 copy-start.7
  104.4 1.4 collective-permute-start.2
  105.8 4.6 %collective-permute-done = bf16[1152,192]{0,1:T(8,128)(2,1)S(1)} collective-permute-done((bf16[1152,192]{0,1:T(8,128)(2,1)S(1)}, bf16[1152,192]{0,1:T(8,128)(2,1)S(1)}, u32[]{:S(2)}, u32[]{:S(2)}) %collective-permute-start) | collective-permute-done | bytes 442400 | tf_op jit(solution)/shard_map/ppermute | solution.py:423
  110.4 9.5 %collective-permute-done.1 = bf16[1152,192]{0,1:T(8,128)(2,1)S(1)} collective-permute-done((bf16[1152,192]{0,1:T(8,128)(2,1)S(1)}, bf16[1152,192]{0,1:T(8,128)(2,1)S(1)}, u32[]{:S(2)}, u32[]{:S(2)}) %collective-permute-start.1) | collective-permute-done | bytes 442400 | tf_op jit(solution)/shard_map/ppermute | solution.py:423
  119.9 9.5 %collective-permute-done.2 = bf16[1152,192]{0,1:T(8,128)(2,1)S(1)} collective-permute-done((bf16[1152,192]{0,1:T(8,128)(2,1)S(1)}, bf16[1152,192]{0,1:T(8,128)(2,1)S(1)}, u32[]{:S(2)}, u32[]{:S(2)}) %collective-permute-start.2) | collective-permute-done | bytes 442400 | tf_op jit(solution)/shard_map/ppermute | solution.py:423
  129.3 0.7 multiply_convert_fusion
  130.0 0.0 copy-start.2
  130.1 0.0 copy-start.3
  130.1 0.0 copy-start.4
  130.1 4.3 %convolution_convert_fusion = bf16[1152,2560]{1,0:T(8,128)(2,1)} fusion(bf16[1152,192]{0,1:T(8,128)(2,1)S(1)} %get-tuple-element.27, bf16[1,192,2560]{2,1,0:T(8,128)(2,1)S(1)} %copy-done), kind=kOutput, calls=%fused_computation.2 | convolution fusion | flops 1135411200 | bytes 7323648 | tf_op jit(solution)/shard_map/dot_general | solution.py:437
  134.3 0.0 copy-done.7
  134.3 1.7 fusion.6
  136.1 0.0 copy-done.2
  136.1 0.0 copy-done.3
  136.1 0.0 copy-done.4
  136.1 4.3 %fusion = bf16[1152,2560]{1,0:T(8,128)(2,1)} fusion(f32[1152,2560]{1,0:T(8,128)S(1)} %fusion.6, bf16[1152,192]{0,1:T(8,128)(2,1)S(1)} %get-tuple-element.25, bf16[1,192,2560]{2,1,0:T(8,128)(2,1)S(1)} %copy-done.8), kind=kOutput, calls=%fused_computation.1 | convolution fusion | flops 1138360320 | bytes 19120128 | tf_op jit(solution)/shard_map/dot_general | solution.py:437
  140.4 85.1 %bring_home.1 = (bf16[2,72,2560]{2,1,0:T(8,128)(2,1)}, bf16[2,72,2560]{2,1,0:T(8,128)(2,1)}, bf16[8,72,2560]{2,1,0:T(8,128)(2,1)}, bf16[8,72,2560]{2,1,0:T(8,128...) custom-call(bf16[16,72,2560]{2,1,0:T(8,128)(2,1)} %bitcast.66, ...), custom_call_target="tpu_custom_call" | custom-call | tf_op jit(solution)/shard_map/bring_home/pallas_call | solution.py:297
  225.5 2.3 convolution_convert_fusion.2.part1
  227.8 2.3 convolution_convert_fusion.3.part0
  230.2 0.0 copy-start.5
  230.2 31.9 %tail_sum.1 = (bf16[128,2560]{1,0:T(8,128)(2,1)}, bf16[128,2560]{1,0:T(8,128)(2,1)}, bf16[4,2,16,2560]{3,2,1,0:T(8,128)(2,1)}, bf16[4,2,16,2560]{3,2,1,0:T(8,128)(2,1)}, bf16[3,2,16,2560]{3,2,1,0:T(8,128)(2,1)}) custom-call(bf16[128,2560]{1,0:T(8,128)(2,1)} %convolution_convert_fusion.3.part0, bf16[128,2560]{1,0:T(8,128)(2,1)} %convolution_convert_fusion.2.part1), custom_call_target="tpu_custom_call" | custom-call | tf_op jit(solution)/shard_map/tail_sum/pallas_call | solution.py:377
  262.1 0.0 copy-start.6
  262.1 2.1 copy.21
  264.2 0.0 copy-start.1
  264.2 2.0 copy.22
  266.3 2.9 %copy.23 = f32[1,192,2560]{2,1,0:T(8,128)} copy(f32[1,192,2560]{2,1,0:T(8,128)} %bitcast.84) | data formatting | bytes 3932160
  269.2 0.0 copy-done.6
  269.2 1.3 copy.24
  270.5 0.0 copy-done.5
  270.5 1.3 copy.25
  271.8 0.0 copy-done.1
  (4 shorter events, 0.0 us)
Async XLA Ops:
  0.6 101.7 %copy-start = (bf16[1,192,2560]{2,1,0:T(8,128)(2,1)S(1)}, bf16[1,192,2560]{2,1,0:T(8,128)(2,1)}, u32[]{:S(2)}) copy-start(bf16[1,192,2560]{2,1,0:T(8,128)(2,1)} %param.12) | copy-start | bytes 2949124
  93.4 6.5 %slice-start = ((s8[5898240]{0:T(1024)(128)(4,1)}), s8[4194304]{0:T(1024)(128)(4,1)S(1)}, s32[]{:S(2)}) async-start(s8[5898240]{0:T(1024)(128)(4,1)} %bitcast.70), calls=%async_computation | async-start | bytes 8388608
  93.4 6.5 %copy-start.8 = (bf16[1,192,2560]{2,1,0:T(8,128)(2,1)S(1)}, bf16[1,192,2560]{2,1,0:T(8,128)(2,1)}, u32[]{:S(2)}) copy-start(bf16[1,192,2560]{2,1,0:T(8,128)(2,1)} %param.11) | copy-start | bytes 2949124
  93.4 6.5 %slice-start.1 = ((s8[5898240]{0:T(1024)(128)(4,1)}), s8[1703936]{0:T(1024)(128)(4,1)S(1)}, s32[]{:S(2)}) async-start(s8[5898240]{0:T(1024)(128)(4,1)} %bitcast.70), calls=%async_computation.1 | async-start | bytes 3407872
  93.4 8.9 %slice-start.2 = ((s8[5898240]{0:T(1024)(128)(4,1)}), s8[4194304]{0:T(1024)(128)(4,1)S(1)}, s32[]{:S(2)}) async-start(s8[5898240]{0:T(1024)(128)(4,1)} %bitcast.74), calls=%async_computation.2 | async-start | bytes 8388608
  98.6 3.8 %slice-start.3 = ((s8[5898240]{0:T(1024)(128)(4,1)}), s8[1703936]{0:T(1024)(128)(4,1)S(1)}, s32[]{:S(2)}) async-start(s8[5898240]{0:T(1024)(128)(4,1)} %bitcast.74), calls=%async_computation.3 | async-start | bytes 3407872
  98.6 11.8 %collective-permute-start = (bf16[1152,192]{0,1:T(8,128)(2,1)S(1)}, bf16[1152,192]{0,1:T(8,128)(2,1)S(1)}, u32[]{:S(2)}, u32[]{:S(2)}) collective-permute-start(bf16[1152,192]{0,1:T(8,128)(2,1)S(1)} %convolution_convert_fusion.6), channel_id=1, source_target_pairs={{0,1},{1,0},{2,3},{3,2},{4,5},{5,4},{6,7},{7,6},{8,9},{9,8},{10,11... | collective-permute-start | bytes 1327112 | tf_op jit(solution)/shard_map/ppermute | solution.py:423
  101.9 18.0 %collective-permute-start.1 = (bf16[1152,192]{0,1:T(8,128)(2,1)S(1)}, bf16[1152,192]{0,1:T(8,128)(2,1)S(1)}, u32[]{:S(2)}, u32[]{:S(2)}) collective-permute-start(bf16[1152,192]{0,1:T(8,128)(2,1)S(1)} %convolution_convert_fusion.5), channel_id=1, source_target_pairs={{0,1},{1,0},{2,3},{3,2},{4,5},{5,4},{6,7},{7,6},{8,9},{9,8},{10,11... | collective-permute-start | bytes 1327112 | tf_op jit(solution)/shard_map/ppermute | solution.py:423
  104.4 30.0 %copy-start.7 = (bf16[1,192,2560]{2,1,0:T(8,128)(2,1)S(1)}, bf16[1,192,2560]{2,1,0:T(8,128)(2,1)}, u32[]{:S(2)}) copy-start(bf16[1,192,2560]{2,1,0:T(8,128)(2,1)} %param.10) | copy-start | bytes 2949124
  104.4 25.0 %collective-permute-start.2 = (bf16[1152,192]{0,1:T(8,128)(2,1)S(1)}, bf16[1152,192]{0,1:T(8,128)(2,1)S(1)}, u32[]{:S(2)}, u32[]{:S(2)}) collective-permute-start(bf16[1152,192]{0,1:T(8,128)(2,1)S(1)} %convolution_convert_fusion.4), channel_id=1, source_target_pairs={{0,1},{1,0},{2,3},{3,2},{4,5},{5,4},{6,7},{7,6},{8,9},{9,8},{10,11... | collective-permute-start | bytes 1327112 | tf_op jit(solution)/shard_map/ppermute | solution.py:423
  130.0 6.0 %copy-start.2 = (bf16[1152,192]{0,1:T(8,128)(2,1)}, bf16[1152,192]{0,1:T(8,128)(2,1)S(1)}, u32[]{:S(2)}) copy-start(bf16[1152,192]{0,1:T(8,128)(2,1)S(1)} %get-tuple-element.27) | copy-start | bytes 1327108
  130.1 6.0 %copy-start.3 = (bf16[1152,192]{0,1:T(8,128)(2,1)}, bf16[1152,192]{0,1:T(8,128)(2,1)S(1)}, u32[]{:S(2)}) copy-start(bf16[1152,192]{0,1:T(8,128)(2,1)S(1)} %get-tuple-element.26) | copy-start | bytes 1327108
  130.1 6.0 %copy-start.4 = (bf16[1152,192]{0,1:T(8,128)(2,1)}, bf16[1152,192]{0,1:T(8,128)(2,1)S(1)}, u32[]{:S(2)}) copy-start(bf16[1152,192]{0,1:T(8,128)(2,1)S(1)} %get-tuple-element.25) | copy-start | bytes 1327108
  230.2 40.3 %copy-start.5 = (f32[192,2560]{1,0:T(8,128)S(1)}, f32[192,2560]{1,0:T(8,128)}, u32[]{:S(2)}) copy-start(f32[192,2560]{1,0:T(8,128)} %get-tuple-element.22) | copy-start | bytes 5898244
  262.1 7.1 %copy-start.6 = (f32[192,2560]{1,0:T(8,128)S(1)}, f32[192,2560]{1,0:T(8,128)}, u32[]{:S(2)}) copy-start(f32[192,2560]{1,0:T(8,128)} %get-tuple-element.21) | copy-start | bytes 5898244
  264.2 7.5 %copy-start.1 = (bf16[1,192,2560]{2,1,0:T(8,128)(2,1)S(1)}, bf16[1,192,2560]{2,1,0:T(8,128)(2,1)}, u32[]{:S(2)}) copy-start(bf16[1,192,2560]{2,1,0:T(8,128)(2,1)} %param.12) | copy-start | bytes 2949124
